TPU v7x, 512 devices: a whole 4x4x16 slice. The times are simulated.
512 devices in a mesh: req: 64 (over x, z), tp: 8 (over y, core).
Axes of the slice: x: 4, y: 4, z: 16, core: 2. Of those that a mesh axis runs over, the one named last changes fastest.
Arguments:
- query_new: bfloat16 [8192, 2048], P('req', 'tp'), may hold values from -6 to 6
- key_new: bfloat16 [8192, 2048], P('req', 'tp'), may hold values from -6 to 6
- value_new: bfloat16 [8192, 2048], P('req', 'tp'), may hold values from -6 to 6
- mlp_hidden: bfloat16 [8192, 8192], P('req', 'tp'), may hold values from -6 to 6
- cache_pages: bfloat16 [4096, 16, 16, 256], P('req', None, 'tp'), may hold values from -6 to 6
- page_dest: int32 [4096, 1], P('req'), may hold values from 0 to 63; in each aligned block of 64 rows (0 to 63, 64 to 127, ...) at most 2 rows name the same one
- page_tag: int32 [4096], P('req'), may hold values from 0 to 3
- seg_ids: int32 [64, 128], P('req'), may hold values from 0 to 3, as said below
- attn_proj: bfloat16 [2048, 4096], P(('tp', 'req')), may hold values from -0.5 to 0.5
- mlp_down: bfloat16 [8192, 4096], P(('tp', 'req')), may hold values from -0.0625 to 0.0625
Outputs:
- layer_out: bfloat16 [8192, 4096], P('req', 'tp')
Inputs may be any that keep to these rules, and one draw needn't show every extreme that they name: `seg_ids`: within each pack the ids never fall; request 0 covers exactly the first 64 tokens and requests 1 to 3 each cover one or more of the rest. `page_dest`: among the rows of one device, at most 2 pages name the same destination, a bound that some block reaches.
All inputs are finite; a program needn't handle non-finite values.
Results may differ from a plain program's by a relative error of at most 0.014.
Values may be sent and summed in bfloat16 or wider, within the bound.
A program may use at most 128 MiB of HBM per device.

v0:
```python
import math

import jax
import jax.numpy as jnp
from jax import lax
from jax.sharding import PartitionSpec as P

HD = 128
ROT = 32
SEG_DEV = 4
CAP = 2


def rotate_heads(values, position, rot_dims):
    half_rot = rot_dims // 2
    frequency = 10000.0 ** (-2.0 * jnp.arange(half_rot, dtype=jnp.float32) / rot_dims)
    angles = position.astype(jnp.float32)[:, None] * frequency[None, :]
    cosine = jnp.cos(angles)[:, None, :]
    sine_part = jnp.sin(angles)[:, None, :]
    leading = values[..., :half_rot]
    trailing = values[..., half_rot:rot_dims]
    return jnp.concatenate(
        [
            leading * cosine - trailing * sine_part,
            trailing * cosine + leading * sine_part,
            values[..., rot_dims:],
        ],
        axis=-1,
    )


def masked_scores(query_rot, block_keys, segment, block_tags, score_scale):
    scores = (
        jnp.einsum("qhd,khd->hqk", query_rot, block_keys, preferred_element_type=jnp.float32)
        * score_scale
    )
    return jnp.where((segment[:, None] == block_tags[None, :])[None], scores, -jnp.inf)


def body(
    query_new,
    key_new,
    value_new,
    mlp_hidden,
    cache_pages,
    page_dest,
    page_tag,
    seg_ids,
    attn_proj,
    mlp_down,
):
    req_count = lax.axis_size("req")
    tok_count = query_new.shape[0]
    heads_local = query_new.shape[1] // HD
    page_rows = cache_pages.shape[1]
    pages_local = cache_pages.shape[0]
    slot_count = req_count * CAP
    score_scale = 1.0 / math.sqrt(HD)
    destination = page_dest[:, 0]
    dest_match = (destination[:, None] == jnp.arange(req_count, dtype=jnp.int32)[None, :]).astype(
        jnp.int32
    )
    earlier = jnp.cumsum(dest_match, axis=0) - dest_match
    rank = jnp.sum(earlier * dest_match, axis=1)
    slot_of_page = destination * CAP + rank
    select = jnp.arange(slot_count, dtype=jnp.int32)[:, None] == slot_of_page[None, :]
    flat_pages = cache_pages.reshape(pages_local, page_rows * heads_local * 2 * HD)
    send_pages = jnp.dot(
        select.astype(jnp.bfloat16), flat_pages, preferred_element_type=jnp.float32
    ).astype(jnp.bfloat16)
    send_pages = send_pages.reshape(req_count, CAP * page_rows, heads_local, 2 * HD)
    send_tags = (
        (jnp.sum(jnp.where(select, page_tag[None, :] + 1, 0), axis=1) - 1)
        .astype(jnp.bfloat16)
        .reshape(req_count, CAP)
    )
    recv_pages, recv_tags = (
        lax.all_to_all(send_pages, "req", split_axis=0, concat_axis=0, tiled=True),
        lax.all_to_all(send_tags, "req", split_axis=0, concat_axis=0, tiled=True),
    )
    slot_pages = recv_pages.reshape(slot_count, page_rows, heads_local, 2 * HD)
    slot_tags = recv_tags.reshape(slot_count).astype(jnp.int32)
    segment = seg_ids[0]
    seg_range = jnp.arange(SEG_DEV, dtype=jnp.int32)
    seg_first = jnp.sum((segment[:, None] < seg_range[None, :]).astype(jnp.int32), axis=0)
    prefix = page_rows * jnp.sum(
        (slot_tags[:, None] == seg_range[None, :]).astype(jnp.int32), axis=0
    )
    seg_match = segment[:, None] == seg_range[None, :]
    offset = jnp.sum(jnp.where(seg_match, prefix[None, :] - seg_first[None, :], 0), axis=1)
    row_index = jnp.arange(tok_count, dtype=jnp.int32)
    position = row_index + offset
    query_rot = rotate_heads(
        query_new.reshape(tok_count, heads_local, HD).astype(jnp.float32), position, ROT
    ).astype(jnp.bfloat16)
    key_rot = rotate_heads(
        key_new.reshape(tok_count, heads_local, HD).astype(jnp.float32), position, ROT
    ).astype(jnp.bfloat16)
    value_heads = value_new.reshape(tok_count, heads_local, HD)
    local_scores = (
        jnp.einsum("qhd,khd->hqk", query_rot, key_rot, preferred_element_type=jnp.float32)
        * score_scale
    )
    causal = (segment[:, None] == segment[None, :]) & (row_index[None, :] <= row_index[:, None])
    local_scores = jnp.where(causal[None], local_scores, -jnp.inf)
    cache_rows = slot_pages.reshape(slot_count * page_rows, heads_local, 2 * HD)
    key_tags = jnp.repeat(slot_tags, page_rows)
    cached = masked_scores(query_rot, cache_rows[..., :HD], segment, key_tags, score_scale)
    row_max = jnp.maximum(jnp.max(local_scores, axis=2), jnp.max(cached, axis=2))
    local_exp = jnp.exp(local_scores - row_max[..., None])
    cached_exp = jnp.exp(cached - row_max[..., None])
    denominator = jnp.sum(local_exp, axis=2) + jnp.sum(cached_exp, axis=2)
    local_weights = (local_exp / denominator[..., None]).astype(jnp.bfloat16)
    cached_weights = (cached_exp / denominator[..., None]).astype(jnp.bfloat16)
    attention = jnp.einsum(
        "hqk,khd->qhd", local_weights, value_heads, preferred_element_type=jnp.float32
    )
    attention = attention + jnp.einsum(
        "hqk,khd->qhd", cached_weights, cache_rows[..., HD:], preferred_element_type=jnp.float32
    )
    attn_flat = attention.astype(jnp.bfloat16).reshape(tok_count, heads_local * HD)
    columns = attn_flat
    attn_part = jnp.dot(
        columns,
        lax.all_gather(attn_proj, "req", axis=0, tiled=True),
        preferred_element_type=jnp.float32,
    )
    columns = mlp_hidden
    partial_value = attn_part + jnp.dot(
        columns,
        lax.all_gather(mlp_down, "req", axis=0, tiled=True),
        preferred_element_type=jnp.float32,
    )
    return lax.psum_scatter(
        partial_value.astype(jnp.bfloat16), "tp", scatter_dimension=1, tiled=True
    )


def solution(mesh):
    return jax.shard_map(
        body,
        mesh=mesh,
        in_specs=(
            P("req", "tp"),
            P("req", "tp"),
            P("req", "tp"),
            P("req", "tp"),
            P("req", None, "tp", None),
            P("req", None),
            P("req"),
            P("req", None),
            P(("tp", "req"), None),
            P(("tp", "req"), None),
        ),
        out_specs=P("req", "tp"),
        check_vma=False,
    )
```

profile of v0, /device:TPU:1, one launch (start us, length us, event | category | flops | bytes accessed | tf_op | source)
XLA Modules:
  0.0 378.2 jit_solution(5007309284389272083)
XLA Ops:
  6.5 0.7 all-gather.6.cloned.1.call-update
  7.3 0.7 all-gather.4.cloned.1.call-update
  8.0 0.7 fusion.17
  8.8 0.8 select_reduce_fusion.1
  9.7 0.7 multiply_add_fusion
  10.5 0.8 convert_element_type.89
  11.3 19.1 %all-to-all-start = ((bf16[64,1,2]{2,1,0:T(2,128)(2,1)}), bf16[64,1,2]{2,1,0:T(2,128)(2,1)S(1)}, u32[]{:S(2)}, u32[]{:S(2)}) async-start(bf16[64,1,2]{2,1,0:T(2,128)(2,1)} %convert_element_type.89), calls=%async_computation | async-start | bytes 65536 | tf_op jit(solution)/shard_map/all_to_all | solution.py:79
  30.4 1.8 reshape.208
  32.2 0.8 convolution_convert_fusion
  33.0 2.8 reshape.209
  35.8 7.8 %all-to-all-done = bf16[64,1,2]{2,1,0:T(2,128)(2,1)S(1)} async-done(((bf16[64,1,2]{2,1,0:T(2,128)(2,1)}), bf16[64,1,2]{2,1,0:T(2,128)(2,1)S(1)}, u32[]{:S(2)}, u32[]{:S(2)}) %all-to-all-start) | async-done | bytes 288 | tf_op jit(solution)/shard_map/all_to_all | solution.py:79
  43.6 7.0 %all-to-all-start.1 = ((bf16[64,32,2,256]{3,2,1,0:T(2,128)(2,1)}), bf16[64,32,2,256]{3,2,1,0:T(2,128)(2,1)S(1)}, u32[]{:S(2)}, u32[]{:S(2)}) async-start(bf16[64,32,2,256]{3,2,1,0:T(2,128)(2,1)} %reshape.209), calls=%async_computation.1 | async-start | bytes 4194304 | tf_op jit(solution)/shard_map/all_to_all | solution.py:78
  50.8 0.1 copy.48
  51.1 0.1 copy.54
  51.4 0.1 copy.62
  51.5 0.1 convert_reduce_fusion.1
  51.9 0.1 reshape.212
  52.2 0.1 multiply_cosine_fusion
  52.7 0.1 subtract_convert_fusion
  52.9 0.3 fusion.20
  53.1 0.2 broadcast_compare_fusion
  53.4 117.2 %all-gather.6.cloned.1.call-done = bf16[64,4,4096]{2,1,0:T(4,128)(2,1)} async-done(((bf16[1,4,4096]{2,1,0:T(4,128)(2,1)}), bf16[64,4,4096]{2,1,0:T(4,128)(2,1)}) %all-gather.6.cloned.1.call-update) | async-done | bytes 2097168 | tf_op jit(solution)/shard_map/all_gather | solution.py:125
  170.6 4.0 %reshape.214 = bf16[256,4096]{1,0:T(8,128)(2,1)} reshape(bf16[64,4,4096]{2,1,0:T(4,128)(2,1)} %all-gather.6.cloned.1.call-done) | data formatting | bytes 4194304
  174.6 0.4 copy.56
  175.1 0.7 fusion.21
  175.9 0.4 fusion.2
  176.3 0.8 convolution_bitcast_fusion.1
  177.1 0.2 fusion.5
  177.3 146.8 %all-gather.4.cloned.1.call-done = bf16[1024,4096]{1,0:T(8,128)(2,1)} async-done(((bf16[16,4096]{1,0:T(8,128)(2,1)}), bf16[1024,4096]{1,0:T(8,128)(2,1)}) %all-gather.4.cloned.1.call-update) | async-done | bytes 8388624 | tf_op jit(solution)/shard_map/all_gather | solution.py:131
  324.1 4.6 %fusion.22 = f32[128,4096]{1,0:T(8,128)S(1)} fusion(bf16[128,1024]{1,0:T(8,128)(2,1)S(1)} %copy-done, bf16[1024,4096]{1,0:T(8,128)(2,1)} %all-gather.4.cloned.1.call-done), kind=kOutput, calls=%fused_computation.58 | convolution fusion | flops 1073741824 | bytes 10747904 | tf_op jit(solution)/shard_map/dot_general | solution.py:129
  328.7 1.5 fusion
  330.3 41.4 %reduce-scatter.2.cloned.1.call-done = bf16[128,512]{1,0:T(8,128)(2,1)} async-done(((bf16[128,4096]{1,0:T(8,128)(2,1)}), bf16[128,512]{1,0:T(8,128)(2,1)}) %reduce-scatter.2.cloned.1.call-update) | async-done | bytes 131088 | tf_op jit(solution)/shard_map/reduce_scatter | solution.py:134
  (40 shorter events, 1.6 us)
Async XLA Ops:
  6.5 317.6 %copy-start = (bf16[128,1024]{1,0:T(8,128)(2,1)S(1)}, bf16[128,1024]{1,0:T(8,128)(2,1)}, u32[]{:S(2)}) copy-start(bf16[128,1024]{1,0:T(8,128)(2,1)} %param.13) | copy-start | bytes 786436
  6.5 164.1 %all-gather.6.cloned.1.call-start = ((), (), s32[]{:S(2)}) async-start(), calls=%async_computation.5 | async-start | bytes 2129920 | tf_op jit(solution)/shard_map/all_gather | solution.py:125
  7.3 316.8 %all-gather.4.cloned.1.call-start = ((), (), s32[]{:S(2)}) async-start(), calls=%async_computation.3 | async-start | bytes 8519680 | tf_op jit(solution)/shard_map/all_gather | solution.py:131
  11.3 32.3 %all-to-all-start = ((bf16[64,1,2]{2,1,0:T(2,128)(2,1)}), bf16[64,1,2]{2,1,0:T(2,128)(2,1)S(1)}, u32[]{:S(2)}, u32[]{:S(2)}) async-start(bf16[64,1,2]{2,1,0:T(2,128)(2,1)} %convert_element_type.89), calls=%async_computation | async-start | bytes 65536 | tf_op jit(solution)/shard_map/all_to_all | solution.py:79
  35.8 14.8 %copy-start.2 = (bf16[128,256]{1,0:T(8,128)(2,1)S(1)}, bf16[128,256]{1,0:T(8,128)(2,1)}, u32[]{:S(2)}) copy-start(bf16[128,256]{1,0:T(8,128)(2,1)} %param.10) | copy-start | bytes 196612
  35.8 15.2 %copy-start.3 = (bf16[128,256]{1,0:T(8,128)(2,1)S(1)}, bf16[128,256]{1,0:T(8,128)(2,1)}, u32[]{:S(2)}) copy-start(bf16[128,256]{1,0:T(8,128)(2,1)} %param.11) | copy-start | bytes 196612
  35.8 15.5 %copy-start.4 = (bf16[128,256]{1,0:T(8,128)(2,1)S(1)}, bf16[128,256]{1,0:T(8,128)(2,1)}, u32[]{:S(2)}) copy-start(bf16[128,256]{1,0:T(8,128)(2,1)} %param.12) | copy-start | bytes 196612
  35.8 15.7 %copy-start.5 = (s32[1,128]{1,0:T(1,128)S(1)}, s32[1,128]{1,0:T(1,128)}, u32[]{:S(2)}) copy-start(s32[1,128]{1,0:T(1,128)} %param.17) | copy-start | bytes 1540
  43.6 131.0 %all-to-all-start.1 = ((bf16[64,32,2,256]{3,2,1,0:T(2,128)(2,1)}), bf16[64,32,2,256]{3,2,1,0:T(2,128)(2,1)S(1)}, u32[]{:S(2)}, u32[]{:S(2)}) async-start(bf16[64,32,2,256]{3,2,1,0:T(2,128)(2,1)} %reshape.209), calls=%async_computation.1 | async-start | bytes 4194304 | tf_op jit(solution)/shard_map/all_to_all | solution.py:78
  50.6 321.1 %reduce-scatter.2.cloned.1.call-start = ((), (), s32[]{:S(2)}) async-start(), calls=%async_computation.4 | async-start | bytes 1179648 | tf_op jit(solution)/shard_map/reduce_scatter | solution.py:134
  177.3 151.5 %copy-start.1 = (bf16[256,4096]{1,0:T(8,128)(2,1)S(1)}, bf16[256,4096]{1,0:T(8,128)(2,1)}, u32[]{:S(2)}) copy-start(bf16[256,4096]{1,0:T(8,128)(2,1)} %reshape.214) | copy-start | bytes 6291460
Sparse Core Ops, SparseCore 0:
  10.3 160.2 all-gather.5
  173.6 150.4 all-gather.3
  330.4 41.2 reduce-scatter.1
where the time goes:
time: 379 us; the launch traced here: 378 us
  waiting for transfers between devices  315 us (83%)
  starting transfers between devices  26.1 us (7%)
  between operations  13.3 us (4%)
  local copies, waits for them, and re-layouts  11.2 us (3%)
  matrix products  8.96 us (2%)
  other arithmetic  4 us (1%)
    all_gather x1, waiting for transfers between devices, body(): lax.all_gather(mlp_down, 'req', axis=0, tiled=True)  147 us
    all_gather x1, waiting for transfers between devices, body(): lax.all_gather(attn_proj, 'req', axis=0, tiled=True)  117 us
    reduce_scatter x1, waiting for transfers between devices, body(): lax.psum_scatter(partial_value.astype(jnp.bfloat16), 'tp', scatter_dimens...  41.4 us
    all_to_all x1, starting transfers between devices, body(): lax.all_to_all(send_tags, 'req', split_axis=0, concat_axis=0, tiled=True)  19.1 us
    all_to_all x1, waiting for transfers between devices, body(): lax.all_to_all(send_tags, 'req', split_axis=0, concat_axis=0, tiled=True)  7.76 us
  transfers between devices with their start and end apart: 5, of which 4 were waited for; matrix products, arithmetic and copies ran while one was open for 5% of the time, Pallas kernels for 0%

commit v1 on v0

--- a/solution.py
+++ b/solution.py
@@ -1,14 +1,198 @@
+import functools
 import math
 
 import jax
 import jax.numpy as jnp
 from jax import lax
+from jax.experimental import pallas as pl
+from jax.experimental.pallas import tpu as pltpu
 from jax.sharding import PartitionSpec as P
 
 HD = 128
 ROT = 32
 SEG_DEV = 4
 CAP = 2
+NX = 4
+MESH = pl.DeviceIdType.MESH
+
+
+def exchange_kernel(count, w_ref, pages_ref, tags_ref, g_ref, rp_ref, rt_ref,
+                    send, zr, zl, xp, xm, relay, psend, precv, tsend, trecv, local):
+    me = lax.axis_index("req")
+    nz = count // NX
+    half_z = nz // 2
+    x = me // nz
+    z = me % nz
+    half = w_ref.shape[1] // 2
+
+    def at(dx, dz):
+        return ((x + dx + NX) % NX) * nz + (z + dz + nz) % nz
+
+    barrier = pltpu.get_barrier_semaphore()
+
+    def greet(i, carry):
+        pl.semaphore_signal(
+            barrier, inc=1, device_id={"req": (me + i) % count}, device_id_type=MESH
+        )
+        return carry
+
+    lax.fori_loop(1, count, greet, 0)
+    pl.semaphore_wait(barrier, count - 1)
+
+    def push(src, dst, recv_sem, to):
+        pltpu.make_async_remote_copy(
+            src_ref=src, dst_ref=dst, send_sem=send.at[0], recv_sem=recv_sem,
+            device_id={"req": to}, device_id_type=MESH,
+        ).start()
+
+    def arrived(ref, sem):
+        pltpu.make_async_copy(ref, ref, sem).wait()
+
+    def page_to(to):
+        pltpu.make_async_remote_copy(
+            src_ref=pages_ref.at[to], dst_ref=rp_ref.at[me], send_sem=psend.at[0],
+            recv_sem=precv.at[0], device_id={"req": to}, device_id_type=MESH,
+        ).start()
+        pltpu.make_async_remote_copy(
+            src_ref=tags_ref.at[to], dst_ref=rt_ref.at[me], send_sem=tsend.at[0],
+            recv_sem=trecv.at[0], device_id={"req": to}, device_id_type=MESH,
+        ).start()
+
+    def pages(dz, first):
+        def one(dx, carry):
+            page_to(at(dx, dz))
+            return carry
+
+        lax.fori_loop(first, NX, one, 0)
+
+    right, left = at(0, 1), at(0, -1)
+    plus, minus = at(1, 0), at(-1, 0)
+
+    def relays(dz, slot):
+        below, above = at(-1, dz), at(1, dz)
+        arrived(g_ref.at[below], xp.at[slot])
+        lo = g_ref.at[below, :, pl.ds(0, half)]
+        push(lo, lo, relay.at[0], plus)
+        arrived(g_ref.at[above], xm.at[slot])
+        hi = g_ref.at[above, :, pl.ds(half, half)]
+        push(hi, hi, relay.at[0], minus)
+
+    push(w_ref, g_ref.at[me], zr.at[0], right)
+    push(w_ref, g_ref.at[me], zl.at[0], left)
+    push(w_ref, g_ref.at[me], xp.at[0], plus)
+    push(w_ref, g_ref.at[me], xm.at[0], minus)
+    own = [
+        pltpu.make_async_copy(w_ref, g_ref.at[me], local.at[0]),
+        pltpu.make_async_copy(pages_ref.at[me], rp_ref.at[me], precv.at[0]),
+        pltpu.make_async_copy(tags_ref.at[me], rt_ref.at[me], trecv.at[0]),
+    ]
+    for copy in own:
+        copy.start()
+    pages(0, 1)
+    for s in range(1, half_z + 1):
+        below = g_ref.at[at(0, -s)]
+        arrived(below, zr.at[s - 1])
+        if s < half_z:
+            push(below, below, zr.at[s], right)
+        push(below, below, xp.at[2 * s - 1], plus)
+        push(below, below, xm.at[2 * s - 1], minus)
+        if s < half_z:
+            above = g_ref.at[at(0, s)]
+            arrived(above, zl.at[s - 1])
+            if s < half_z - 1:
+                push(above, above, zl.at[s], left)
+            push(above, above, xp.at[2 * s], plus)
+            push(above, above, xm.at[2 * s], minus)
+        pages(s, 0)
+        if s < half_z:
+            pages(-s, 0)
+        if s == 1:
+            relays(0, 0)
+        else:
+            relays(-(s - 1), 2 * s - 3)
+            relays(s - 1, 2 * s - 2)
+    relays(-half_z, 2 * half_z - 1)
+    own[0].wait()
+    arrived(g_ref.at[pl.ds(0, nz)], relay.at[0])
+    arrived(g_ref.at[pl.ds(0, count - 1)], send.at[0])
+    arrived(rp_ref, precv.at[0])
+    arrived(rt_ref, trecv.at[0])
+    arrived(rp_ref.at[pl.ds(0, count - 1)], psend.at[0])
+    arrived(rt_ref.at[pl.ds(0, count - 1)], tsend.at[0])
+
+
+def exchange(weights, send_pages, send_tags):
+    count = send_pages.shape[0]
+    half_z = count // NX // 2
+    any_space = pl.BlockSpec(memory_space=pl.ANY)
+    dma = pltpu.SemaphoreType.DMA
+    return pl.pallas_call(
+        functools.partial(exchange_kernel, count),
+        out_shape=(
+            jax.ShapeDtypeStruct((count,) + weights.shape, weights.dtype),
+            jax.ShapeDtypeStruct(send_pages.shape, send_pages.dtype),
+            jax.ShapeDtypeStruct(send_tags.shape, send_tags.dtype),
+        ),
+        in_specs=[pl.BlockSpec(memory_space=pltpu.VMEM)] * 3,
+        out_specs=(any_space, any_space, any_space),
+        scratch_shapes=[
+            dma((1,)), dma((half_z,)), dma((half_z,)), dma((2 * half_z,)), dma((2 * half_z,)),
+            dma((1,)), dma((1,)), dma((1,)), dma((1,)), dma((1,)), dma((1,)),
+        ],
+        compiler_params=pltpu.CompilerParams(collective_id=0, has_side_effects=True),
+        name="exchange",
+    )(weights, send_pages, send_tags)
+
+
+def reduce_kernel(count, part_ref, out_ref, held, send, recv):
+    me = lax.axis_index("tp")
+    width = out_ref.shape[1]
+    barrier = pltpu.get_barrier_semaphore()
+    for i in range(1, count):
+        pl.semaphore_signal(
+            barrier, inc=1, device_id={"tp": (me + i) % count}, device_id_type=MESH
+        )
+    pl.semaphore_wait(barrier, count - 1)
+
+    def columns(g):
+        return part_ref.at[:, pl.ds(pl.multiple_of(g * width, width), width)]
+
+    copies = []
+    for i in range(1, count):
+        to = (me + i) % count
+        copies.append(
+            pltpu.make_async_remote_copy(
+                src_ref=columns(to), dst_ref=held.at[i - 1], send_sem=send.at[i - 1],
+                recv_sem=recv.at[i - 1], device_id={"tp": to}, device_id_type=MESH,
+            )
+        )
+        copies[-1].start()
+    total = columns(me)[...].astype(jnp.float32)
+    for i, copy in enumerate(copies):
+        copy.wait_recv()
+        total = total + held[i].astype(jnp.float32)
+    out_ref[...] = total.astype(out_ref.dtype)
+    for copy in copies:
+        copy.wait_send()
+
+
+def reduce_groups(partial_value):
+    count = lax.axis_size("tp")
+    rows, columns = partial_value.shape
+    width = columns // count
+    return pl.pallas_call(
+        functools.partial(reduce_kernel, count),
+        out_shape=jax.ShapeDtypeStruct((rows, width), partial_value.dtype),
+        in_specs=[pl.BlockSpec(memory_space=pltpu.VMEM)],
+        out_specs=pl.BlockSpec(memory_space=pltpu.VMEM),
+        scratch_shapes=[
+            pltpu.VMEM((count - 1, rows, width), partial_value.dtype),
+            pltpu.SemaphoreType.DMA((count - 1,)),
+            pltpu.SemaphoreType.DMA((count - 1,)),
+        ],
+        compiler_params=pltpu.CompilerParams(collective_id=1, has_side_effects=True),
+        name="reduce_groups",
+    )(partial_value)
 
 
 def rotate_heads(values, position, rot_dims):
@@ -31,7 +215,7 @@
 
 def masked_scores(query_rot, block_keys, segment, block_tags, score_scale):
     scores = (
-        jnp.einsum("qhd,khd->hqk", query_rot, block_keys, preferred_element_type=jnp.float32)
+        jnp.einsum("qhd,hkd->hqk", query_rot, block_keys, preferred_element_type=jnp.float32)
         * score_scale
     )
     return jnp.where((segment[:, None] == block_tags[None, :])[None], scores, -jnp.inf)
@@ -68,18 +252,18 @@
     send_pages = jnp.dot(
         select.astype(jnp.bfloat16), flat_pages, preferred_element_type=jnp.float32
     ).astype(jnp.bfloat16)
-    send_pages = send_pages.reshape(req_count, CAP * page_rows, heads_local, 2 * HD)
+    blocks = 2 * heads_local
+    send_pages = (
+        send_pages.reshape(req_count, CAP * page_rows, blocks, HD).transpose(0, 2, 1, 3)
+    )
     send_tags = (
-        (jnp.sum(jnp.where(select, page_tag[None, :] + 1, 0), axis=1) - 1)
-        .astype(jnp.bfloat16)
-        .reshape(req_count, CAP)
-    )
-    recv_pages, recv_tags = (
-        lax.all_to_all(send_pages, "req", split_axis=0, concat_axis=0, tiled=True),
-        lax.all_to_all(send_tags, "req", split_axis=0, concat_axis=0, tiled=True),
-    )
-    slot_pages = recv_pages.reshape(slot_count, page_rows, heads_local, 2 * HD)
-    slot_tags = recv_tags.reshape(slot_count).astype(jnp.int32)
+        jnp.sum(jnp.where(select, page_tag[None, :] + 1, 0), axis=1) - 1
+    ).reshape(req_count, 1, CAP)
+    send_tags = jnp.pad(send_tags, ((0, 0), (0, 0), (0, HD - CAP)))
+    shard_rows, width = mlp_down.shape
+    weights = jnp.concatenate([mlp_down, attn_proj.reshape(shard_rows, -1)], axis=1)
+    gathered, recv_pages, recv_tags = exchange(weights, send_pages, send_tags)
+    slot_tags = recv_tags[:, 0, :CAP].reshape(slot_count)
     segment = seg_ids[0]
     seg_range = jnp.arange(SEG_DEV, dtype=jnp.int32)
     seg_first = jnp.sum((segment[:, None] < seg_range[None, :]).astype(jnp.int32), axis=0)
@@ -103,9 +287,12 @@
     )
     causal = (segment[:, None] == segment[None, :]) & (row_index[None, :] <= row_index[:, None])
     local_scores = jnp.where(causal[None], local_scores, -jnp.inf)
-    cache_rows = slot_pages.reshape(slot_count * page_rows, heads_local, 2 * HD)
+    cache_rows = recv_pages.reshape(req_count, heads_local, 2, CAP * page_rows, HD)
+    cache_rows = cache_rows.transpose(2, 1, 0, 3, 4).reshape(
+        2, heads_local, slot_count * page_rows, HD
+    )
     key_tags = jnp.repeat(slot_tags, page_rows)
-    cached = masked_scores(query_rot, cache_rows[..., :HD], segment, key_tags, score_scale)
+    cached = masked_scores(query_rot, cache_rows[0], segment, key_tags, score_scale)
     row_max = jnp.maximum(jnp.max(local_scores, axis=2), jnp.max(cached, axis=2))
     local_exp = jnp.exp(local_scores - row_max[..., None])
     cached_exp = jnp.exp(cached - row_max[..., None])
@@ -116,24 +303,21 @@
         "hqk,khd->qhd", local_weights, value_heads, preferred_element_type=jnp.float32
     )
     attention = attention + jnp.einsum(
-        "hqk,khd->qhd", cached_weights, cache_rows[..., HD:], preferred_element_type=jnp.float32
+        "hqk,hkd->qhd", cached_weights, cache_rows[1], preferred_element_type=jnp.float32
     )
     attn_flat = attention.astype(jnp.bfloat16).reshape(tok_count, heads_local * HD)
-    columns = attn_flat
+    proj_rows = attn_flat.shape[1]
     attn_part = jnp.dot(
-        columns,
-        lax.all_gather(attn_proj, "req", axis=0, tiled=True),
+        attn_flat,
+        gathered[:, :, width:].reshape(proj_rows, width),
         preferred_element_type=jnp.float32,
     )
-    columns = mlp_hidden
     partial_value = attn_part + jnp.dot(
-        columns,
-        lax.all_gather(mlp_down, "req", axis=0, tiled=True),
+        mlp_hidden,
+        gathered[:, :, :width].reshape(req_count * shard_rows, width),
         preferred_element_type=jnp.float32,
     )
-    return lax.psum_scatter(
-        partial_value.astype(jnp.bfloat16), "tp", scatter_dimension=1, tiled=True
-    )
+    return reduce_groups(partial_value.astype(jnp.bfloat16))
 
 
 def solution(mesh):

time: 379 us -> 221 us (0.58)
  waiting for transfers between devices: 315 us -> 0 us
  Pallas kernels: 0 us -> 166 us
  starting transfers between devices: 26.1 us -> 0 us
  local copies, waits for them, and re-layouts: 11.2 us -> 31.8 us
  between operations: 13.3 us -> 0.25 us
  other arithmetic: 4 us -> 8.61 us
  matrix products: 8.96 us -> 13 us
    all_gather x2 -> x0, waiting for transfers between devices: 264 us -> none  [the longest x1 147 us: body(): lax.all_gather(mlp_down, 'req', axis=0, tiled=True)]
    pallas_call x0 -> x2, Pallas kernels: none -> 166 us  [the longest x1 140 us: exchange(): pl.pallas_call(functools.partial(exchange_kernel, count), out_shape=(jax....]
    reduce_scatter x1 -> x0, waiting for transfers between devices: 41.4 us -> none  [body(): lax.psum_scatter(partial_value.astype(jnp.bfloat16), 'tp', scatter_dimens...]
    all_to_all x2 -> x0, starting transfers between devices: 26.1 us -> none  [the longest x1 19.1 us: body(): lax.all_to_all(send_tags, 'req', split_axis=0, concat_axis=0, tiled=True)]
    slice x0 -> x4, local copies, waits for them, and re-layouts: none -> 10.8 us  [the longest x1 7.83 us: body(): gathered[:, :, :width].reshape(req_count * shard_rows, width)]
    reshape x1 -> x5, local copies, waits for them, and re-layouts: 2.81 us -> 11.6 us  [the longest x2 6.2 us: body(): send_pages.reshape(req_count, CAP * page_rows, blocks, HD)]
    all_to_all x2 -> x0, waiting for transfers between devices: 7.76 us -> none  [the longest x1 7.76 us: body(): lax.all_to_all(send_tags, 'req', split_axis=0, concat_axis=0, tiled=True)]
  transfers between devices with their start and end apart: 5 -> 0, of which waited for: 4 -> 0; matrix products, arithmetic and copies ran while one was open for 5% -> 0% of each run, Pallas kernels for 0% -> 0%
where the time goes in v1:
time: 221 us; the launch traced here: 220 us
  Pallas kernels  166 us (75%)
  local copies, waits for them, and re-layouts  31.8 us (14%)
  matrix products  13 us (6%)
  other arithmetic  8.61 us (4%)
    pallas_call x1, Pallas kernels, exchange(): pl.pallas_call(functools.partial(exchange_kernel, count), out_shape=(jax....  140 us
    pallas_call x1, Pallas kernels, reduce_groups(): pl.pallas_call(functools.partial(reduce_kernel, count), out_shape=jax.Sha...  25.9 us
    slice x1, local copies, waits for them, and re-layouts, body(): gathered[:, :, :width].reshape(req_count * shard_rows, width)  7.83 us
    reshape x2, local copies, waits for them, and re-layouts, body(): send_pages.reshape(req_count, CAP * page_rows, blocks, HD)  6.2 us
    dot_general x1, matrix products, body(): jnp.dot(mlp_hidden, gathered[:, :, :width].reshape(req_count * shard_rows...  6 us

profile of v1, /device:TPU:1, one launch (start us, length us, event | category | flops | bytes accessed | tf_op | source)
XLA Modules:
  0.0 220.1 jit_solution(9224147705309736887)
XLA Ops:
  0.0 1.4 convert_reduce_fusion
  1.4 0.5 multiply_power_fusion
  1.9 0.8 fusion.14
  2.8 0.8 reshape.209
  3.5 0.7 fusion.15
  4.4 0.8 select_reduce_fusion.1
  5.2 0.7 multiply_add_fusion
  6.6 0.6 pad.4.tags_ref
  7.2 0.9 copy.43
  8.3 0.7 slice.50
  9.0 1.0 copy.50
  10.1 0.7 slice.53
  10.8 0.7 convert_element_type.55
  11.5 1.6 copy.61
  13.1 1.6 pad_maximum_fusion.w_ref
  14.6 0.8 reshape.210
  15.5 1.4 convolution_convert_fusion
  16.9 2.7 %reshape.211 = bf16[64,32,4,128]{3,2,1,0:T(4,128)(2,1)} reshape(bf16[128,8192]{1,0:T(8,128)(2,1)S(1)} %convolution_convert_fusion) | data formatting | bytes 4194304 | tf_op jit(solution)/shard_map/reshape | solution.py:257
  19.6 3.5 %copy.65 = bf16[64,32,4,128]{3,1,2,0:T(8,128)(2,1)} copy(bf16[64,32,4,128]{3,2,1,0:T(4,128)(2,1)} %reshape.211) | data formatting | bytes 4194304 | tf_op jit(solution)/shard_map/reshape | solution.py:257
  23.1 140.5 %exchange.1 = (bf16[64,16,5120]{2,1,0:T(8,128)(2,1)}, bf16[64,4,32,128]{3,2,1,0:T(8,128)(2,1)}, s32[64,1,128]{2,1,0:T(1,128)}) custom-call(bf16[16,5120]{1,0:T(8,128)(2,1)} %pad_maximum_fusion.w_ref, bf16[64,4,32,128]{3,2,1,0:T(8,128)(2,1)} %bitcast.37, s32[64,1,128]{2,1,0:T(1,128)} %pad.4.tags_ref), custom_call_target="tpu_custom_call" | custom-call | tf_op jit(solution)/shard_map/exchange/pallas_call | solution.py:129
  163.6 0.8 slice_reduce_fusion
  164.6 2.0 copy.64
  168.5 0.7 fusion.20
  169.2 0.4 fusion.2
  169.7 0.8 convolution_bitcast_fusion.2
  170.7 1.8 slice.46
  172.5 7.8 %slice.47 = bf16[64,16,4096]{2,1,0:T(8,128)(2,1)} slice(bf16[64,16,5120]{2,1,0:T(8,128)(2,1)} %get-tuple-element.10), slice={[0:64], [0:16], [0:4096]} | slice | bytes 16777216 | tf_op jit(solution)/shard_map/slice | solution.py:317
  180.4 6.0 %convolution_bitcast_fusion = f32[128,4096]{1,0:T(8,128)} fusion(bf16[128,1024]{1,0:T(8,128)(2,1)S(1)} %copy-done, bf16[1024,4096]{1,0:T(8,128)(2,1)} %bitcast.36), kind=kOutput, calls=%fused_computation.1 | convolution fusion | flops 1073741824 | bytes 10747904 | tf_op jit(solution)/shard_map/dot_general | solution.py:315
  186.4 2.6 %reshape.215 = bf16[256,4096]{1,0:T(8,128)(2,1)} reshape(bf16[64,16,1024]{2,1,0:T(8,128)(2,1)S(1)} %slice.46) | data formatting | bytes 4194304 | tf_op jit(solution)/shard_map/reshape | solution.py:312
  188.9 3.7 %fusion.part_ref = bf16[128,4096]{1,0:T(8,128)(2,1)} fusion(f32[128,4096]{1,0:T(8,128)} %convolution_bitcast_fusion, bf16[128,256]{0,1:T(8,128)(2,1)S(1)} %bitcast.46, bf16[256,4096]{1,0:T(8,128)(2,1)} %reshape.215), kind=kOutput, calls=%fused_computation.3 | convolution fusion | flops 269484032 | bytes 5308416 | tf_op jit(solution)/shard_map/dot_general | solution.py:310
  192.6 25.9 %reduce_groups.1 = bf16[128,512]{1,0:T(8,128)(2,1)} custom-call(bf16[128,4096]{1,0:T(8,128)(2,1)} %fusion.part_ref), custom_call_target="tpu_custom_call" | custom-call | tf_op jit(solution)/shard_map/reduce_groups/pallas_call | solution.py:183
  218.5 1.6 copy.67
  (45 shorter events, 3.3 us)
Async XLA Ops:
  0.0 180.4 %copy-start = (bf16[128,1024]{1,0:T(8,128)(2,1)S(1)}, bf16[128,1024]{1,0:T(8,128)(2,1)}, u32[]{:S(2)}) copy-start(bf16[128,1024]{1,0:T(8,128)(2,1)} %param.13) | copy-start | bytes 786436
  0.0 14.6 %copy-start.2 = (bf16[64,16,2,256]{3,2,1,0:T(2,128)(2,1)S(1)}, bf16[64,16,2,256]{3,2,1,0:T(2,128)(2,1)}, u32[]{:S(2)}) copy-start(bf16[64,16,2,256]{3,2,1,0:T(2,128)(2,1)} %param.14) | copy-start | bytes 3145732
  5.9 0.5 copy-start.7
  166.6 0.6 copy-start.9
  166.6 0.7 copy-start.6
  166.6 0.7 copy-start.8
  166.6 1.2 copy-start.1
  166.6 1.4 copy-start.3
  166.6 1.4 copy-start.4
  169.7 0.8 copy-start.5

commit v2 on v1

v2 whole, which is shorter than its diff:
```python
import functools
import math

import jax
import jax.numpy as jnp
from jax import lax
from jax.experimental import pallas as pl
from jax.experimental.pallas import tpu as pltpu
from jax.sharding import PartitionSpec as P

HD = 128
ROT = 32
SEG_DEV = 4
CAP = 2
NX = 4
MESH = pl.DeviceIdType.MESH


def exchange_kernel(count, w_ref, p_ref, h_ref, pages_ref, tags_ref, g_ref, ha_ref, rp_ref, rt_ref,
                    send, zr, zl, xp, xm, relay, psend, precv, tsend, trecv, wsend, wrecv,
                    hsend, hrecv):
    me = lax.axis_index("req")
    tp = lax.axis_index("tp")
    groups = ha_ref.shape[0]
    nz = count // NX
    half_z = nz // 2
    x = me // nz
    z = me % nz
    rows, proj = w_ref.shape[0], p_ref.shape[2]
    width = w_ref.shape[1] // groups

    def at(dx, dz):
        return ((x + dx + NX) % NX) * nz + (z + dz + nz) % nz

    def shard(owner, first=0, size=groups):
        return g_ref.at[pl.ds(first, size), pl.ds(pl.multiple_of(owner * rows, rows), rows), :]

    def shards(number):
        return g_ref.at[:, pl.ds(0, number * rows), :]

    barrier = pltpu.get_barrier_semaphore()

    def greet_tp(i, carry):
        pl.semaphore_signal(
            barrier, inc=1, device_id={"tp": (tp + i) % groups}, device_id_type=MESH
        )
        return carry

    def greet(i, carry):
        pl.semaphore_signal(
            barrier, inc=1, device_id={"req": (me + i) % count}, device_id_type=MESH
        )
        return carry

    lax.fori_loop(1, groups, greet_tp, 0)
    lax.fori_loop(1, count, greet, 0)
    pl.semaphore_wait(barrier, count + groups - 2)

    def push(ref, recv_sem, to):
        pltpu.make_async_remote_copy(
            src_ref=ref, dst_ref=ref, send_sem=send.at[0], recv_sem=recv_sem,
            device_id={"req": to}, device_id_type=MESH,
        ).start()

    def arrived(ref, sem):
        pltpu.make_async_copy(ref, ref, sem).wait()

    own = pl.ds(pl.multiple_of(me * rows, rows), rows)
    down_slot = g_ref.at[tp, own, pl.ds(0, width)]
    proj_slot = g_ref.at[tp, own, pl.ds(width, proj)]

    def down_of(g):
        return w_ref.at[:, pl.ds(pl.multiple_of(g * width, width), width)]

    def columns_to(i, carry):
        to = (tp + i) % groups
        for src, dst in ((down_of(to), down_slot), (p_ref.at[to], proj_slot)):
            pltpu.make_async_remote_copy(
                src_ref=src, dst_ref=dst, send_sem=wsend.at[0], recv_sem=wrecv.at[0],
                device_id={"tp": to}, device_id_type=MESH,
            ).start()
        return carry

    def hidden_to(i, carry):
        pltpu.make_async_remote_copy(
            src_ref=h_ref, dst_ref=ha_ref.at[tp], send_sem=hsend.at[0], recv_sem=hrecv.at[0],
            device_id={"tp": (tp + i) % groups}, device_id_type=MESH,
        ).start()
        return carry

    def pages(dz, first):
        def one(dx, carry):
            to = at(dx, dz)
            pltpu.make_async_remote_copy(
                src_ref=pages_ref.at[to], dst_ref=rp_ref.at[me], send_sem=psend.at[0],
                recv_sem=precv.at[0], device_id={"req": to}, device_id_type=MESH,
            ).start()
            pltpu.make_async_remote_copy(
                src_ref=tags_ref.at[to], dst_ref=rt_ref.at[me], send_sem=tsend.at[0],
                recv_sem=trecv.at[0], device_id={"req": to}, device_id_type=MESH,
            ).start()
            return carry

        lax.fori_loop(first, NX, one, 0)

    lax.fori_loop(1, groups, columns_to, 0)
    pltpu.make_async_copy(down_of(tp), down_slot, wrecv.at[0]).start()
    pltpu.make_async_copy(p_ref.at[tp], proj_slot, wrecv.at[0]).start()
    pages(0, 1)
    lax.fori_loop(1, groups, hidden_to, 0)
    pltpu.make_async_copy(h_ref, ha_ref.at[tp], hrecv.at[0]).start()
    pltpu.make_async_copy(pages_ref.at[me], rp_ref.at[me], precv.at[0]).start()
    pltpu.make_async_copy(tags_ref.at[me], rt_ref.at[me], trecv.at[0]).start()

    right, left = at(0, 1), at(0, -1)
    plus, minus = at(1, 0), at(-1, 0)

    def relays(dz, slot):
        below, above = at(-1, dz), at(1, dz)
        arrived(shard(below), xp.at[slot])
        push(shard(below, 0, groups // 2), relay.at[0], plus)
        arrived(shard(above), xm.at[slot])
        push(shard(above, groups // 2, groups // 2), relay.at[0], minus)

    mine = shard(me)
    arrived(mine, wrecv.at[0])
    push(mine, zr.at[0], right)
    push(mine, zl.at[0], left)
    push(mine, xp.at[0], plus)
    push(mine, xm.at[0], minus)
    for s in range(1, half_z + 1):
        below = shard(at(0, -s))
        arrived(below, zr.at[s - 1])
        if s < half_z:
            push(below, zr.at[s], right)
        push(below, xp.at[2 * s - 1], plus)
        push(below, xm.at[2 * s - 1], minus)
        if s < half_z:
            above = shard(at(0, s))
            arrived(above, zl.at[s - 1])
            if s < half_z - 1:
                push(above, zl.at[s], left)
            push(above, xp.at[2 * s], plus)
            push(above, xm.at[2 * s], minus)
        pages(s, 0)
        if s < half_z:
            pages(-s, 0)
        if s == 1:
            relays(0, 0)
        else:
            relays(-(s - 1), 2 * s - 3)
            relays(s - 1, 2 * s - 2)
    relays(-half_z, 2 * half_z - 1)
    arrived(shards(nz), relay.at[0])
    arrived(shards(count - 1), send.at[0])
    arrived(rp_ref, precv.at[0])
    arrived(rt_ref, trecv.at[0])
    arrived(ha_ref, hrecv.at[0])
    arrived(rp_ref.at[pl.ds(0, count - 1)], psend.at[0])
    arrived(rt_ref.at[pl.ds(0, count - 1)], tsend.at[0])
    arrived(ha_ref.at[pl.ds(0, groups - 1)], hsend.at[0])
    arrived(g_ref.at[pl.ds(0, groups - 1), pl.ds(0, rows), :], wsend.at[0])


def exchange(down, proj, hidden, send_pages, send_tags):
    count = send_pages.shape[0]
    groups = proj.shape[0]
    half_z = count // NX // 2
    any_space = pl.BlockSpec(memory_space=pl.ANY)
    dma = pltpu.SemaphoreType.DMA
    rows = down.shape[0]
    width = down.shape[1] // groups + proj.shape[2]
    return pl.pallas_call(
        functools.partial(exchange_kernel, count),
        out_shape=(
            jax.ShapeDtypeStruct((groups, count * rows, width), down.dtype),
            jax.ShapeDtypeStruct((groups,) + hidden.shape, hidden.dtype),
            jax.ShapeDtypeStruct(send_pages.shape, send_pages.dtype),
            jax.ShapeDtypeStruct(send_tags.shape, send_tags.dtype),
        ),
        in_specs=[pl.BlockSpec(memory_space=pltpu.VMEM)] * 5,
        out_specs=(any_space,) * 4,
        scratch_shapes=[
            dma((1,)), dma((half_z,)), dma((half_z,)), dma((2 * half_z,)), dma((2 * half_z,)),
        ] + [dma((1,))] * 9,
        compiler_params=pltpu.CompilerParams(collective_id=0, has_side_effects=True),
        name="exchange",
    )(down, proj, hidden, send_pages, send_tags)


def spread_kernel(groups, part_ref, out_ref, send, recv):
    me = lax.axis_index("tp")
    barrier = pltpu.get_barrier_semaphore()
    for i in range(1, groups):
        pl.semaphore_signal(
            barrier, inc=1, device_id={"tp": (me + i) % groups}, device_id_type=MESH
        )
    pl.semaphore_wait(barrier, groups - 1)
    for i in range(1, groups):
        pltpu.make_async_remote_copy(
            src_ref=part_ref, dst_ref=out_ref.at[me], send_sem=send, recv_sem=recv,
            device_id={"tp": (me + i) % groups}, device_id_type=MESH,
        ).start()
    pltpu.make_async_copy(part_ref, out_ref.at[me], recv).start()
    pltpu.make_async_copy(out_ref, out_ref, recv).wait()
    rest = out_ref.at[pl.ds(0, groups - 1)]
    pltpu.make_async_copy(rest, rest, send).wait()


def spread(part):
    groups = lax.axis_size("tp")
    return pl.pallas_call(
        functools.partial(spread_kernel, groups),
        out_shape=jax.ShapeDtypeStruct((groups,) + part.shape, part.dtype),
        in_specs=[pl.BlockSpec(memory_space=pltpu.VMEM)],
        out_specs=pl.BlockSpec(memory_space=pltpu.VMEM),
        scratch_shapes=[pltpu.SemaphoreType.DMA, pltpu.SemaphoreType.DMA],
        compiler_params=pltpu.CompilerParams(collective_id=1, has_side_effects=True),
        name="spread",
    )(part)


def project_kernel(fold, h_ref, a_ref, down_ref, proj_ref, out_ref, total, wide, flat):
    group = pl.program_id(0)
    lanes = proj_ref.shape[2]
    depth = a_ref.shape[2]
    wide[...] = proj_ref[0].astype(jnp.float32)
    for c in range(fold):
        flat[:, c * lanes:(c + 1) * lanes] = wide[pl.ds(c, depth, stride=fold), :].astype(flat.dtype)
    term = jnp.dot(h_ref[0], down_ref[0], preferred_element_type=jnp.float32)
    term = term + jnp.dot(a_ref[0], flat[...], preferred_element_type=jnp.float32)

    @pl.when(group == 0)
    def _():
        total[...] = term

    @pl.when(group > 0)
    def _():
        total[...] += term

    @pl.when(group == pl.num_programs(0) - 1)
    def _():
        out_ref[...] = total[...].astype(out_ref.dtype)


def project(hidden, attention, gathered, width):
    groups, tokens, units = hidden.shape
    depth = attention.shape[2]
    lanes = gathered.shape[2] - width
    fold = width // lanes

    def block(rows, columns, at=0):
        return pl.BlockSpec((1, rows, columns), lambda g: (g, 0, at))

    return pl.pallas_call(
        functools.partial(project_kernel, fold),
        out_shape=jax.ShapeDtypeStruct((tokens, width), hidden.dtype),
        grid=(groups,),
        in_specs=[
            block(tokens, units),
            block(tokens, depth),
            block(units, width),
            block(units, lanes, fold),
        ],
        out_specs=pl.BlockSpec((tokens, width), lambda g: (0, 0)),
        scratch_shapes=[
            pltpu.VMEM((tokens, width), jnp.float32),
            pltpu.VMEM((units, lanes), jnp.float32),
            pltpu.VMEM((depth, width), hidden.dtype),
        ],
        name="project",
    )(hidden, attention, gathered, gathered)


def rotate_heads(values, position, rot_dims):
    half_rot = rot_dims // 2
    frequency = 10000.0 ** (-2.0 * jnp.arange(half_rot, dtype=jnp.float32) / rot_dims)
    angles = position.astype(jnp.float32)[:, None] * frequency[None, :]
    cosine = jnp.cos(angles)[:, None, :]
    sine_part = jnp.sin(angles)[:, None, :]
    leading = values[..., :half_rot]
    trailing = values[..., half_rot:rot_dims]
    return jnp.concatenate(
        [
            leading * cosine - trailing * sine_part,
            trailing * cosine + leading * sine_part,
            values[..., rot_dims:],
        ],
        axis=-1,
    )


def masked_scores(query_rot, block_keys, segment, block_tags, score_scale):
    scores = (
        jnp.einsum("qhd,hkd->hqk", query_rot, block_keys, preferred_element_type=jnp.float32)
        * score_scale
    )
    return jnp.where((segment[:, None] == block_tags[None, :])[None], scores, -jnp.inf)


def body(
    query_new,
    key_new,
    value_new,
    mlp_hidden,
    cache_pages,
    page_dest,
    page_tag,
    seg_ids,
    attn_proj,
    mlp_down,
):
    req_count = lax.axis_size("req")
    tok_count = query_new.shape[0]
    heads_local = query_new.shape[1] // HD
    page_rows = cache_pages.shape[1]
    pages_local = cache_pages.shape[0]
    slot_count = req_count * CAP
    score_scale = 1.0 / math.sqrt(HD)
    destination = page_dest[:, 0]
    dest_match = (destination[:, None] == jnp.arange(req_count, dtype=jnp.int32)[None, :]).astype(
        jnp.int32
    )
    earlier = jnp.cumsum(dest_match, axis=0) - dest_match
    rank = jnp.sum(earlier * dest_match, axis=1)
    slot_of_page = destination * CAP + rank
    select = jnp.arange(slot_count, dtype=jnp.int32)[:, None] == slot_of_page[None, :]
    flat_pages = cache_pages.reshape(pages_local, page_rows * heads_local * 2 * HD)
    send_pages = jnp.dot(
        select.astype(jnp.bfloat16), flat_pages, preferred_element_type=jnp.float32
    ).astype(jnp.bfloat16)
    blocks = 2 * heads_local
    send_pages = (
        send_pages.reshape(req_count, CAP * page_rows, blocks, HD).transpose(0, 2, 1, 3)
    )
    send_tags = (
        jnp.sum(jnp.where(select, page_tag[None, :] + 1, 0), axis=1) - 1
    ).reshape(req_count, 1, CAP)
    send_tags = jnp.pad(send_tags, ((0, 0), (0, 0), (0, HD - CAP)))
    groups = lax.axis_size("tp")
    shard_rows = mlp_down.shape[0]
    proj_rows = attn_proj.shape[0]
    width = mlp_down.shape[1] // groups
    proj = attn_proj.reshape(proj_rows, groups, shard_rows // proj_rows, -1)
    proj = proj.transpose(1, 0, 2, 3).reshape(groups, shard_rows, -1)
    gathered, hidden, recv_pages, recv_tags = exchange(
        mlp_down, proj, mlp_hidden, send_pages, send_tags
    )
    slot_tags = recv_tags[:, 0, :CAP].reshape(slot_count)
    segment = seg_ids[0]
    seg_range = jnp.arange(SEG_DEV, dtype=jnp.int32)
    seg_first = jnp.sum((segment[:, None] < seg_range[None, :]).astype(jnp.int32), axis=0)
    prefix = page_rows * jnp.sum(
        (slot_tags[:, None] == seg_range[None, :]).astype(jnp.int32), axis=0
    )
    seg_match = segment[:, None] == seg_range[None, :]
    offset = jnp.sum(jnp.where(seg_match, prefix[None, :] - seg_first[None, :], 0), axis=1)
    row_index = jnp.arange(tok_count, dtype=jnp.int32)
    position = row_index + offset
    query_rot = rotate_heads(
        query_new.reshape(tok_count, heads_local, HD).astype(jnp.float32), position, ROT
    ).astype(jnp.bfloat16)
    key_rot = rotate_heads(
        key_new.reshape(tok_count, heads_local, HD).astype(jnp.float32), position, ROT
    ).astype(jnp.bfloat16)
    value_heads = value_new.reshape(tok_count, heads_local, HD)
    local_scores = (
        jnp.einsum("qhd,khd->hqk", query_rot, key_rot, preferred_element_type=jnp.float32)
        * score_scale
    )
    causal = (segment[:, None] == segment[None, :]) & (row_index[None, :] <= row_index[:, None])
    local_scores = jnp.where(causal[None], local_scores, -jnp.inf)
    cache_rows = recv_pages.reshape(req_count, heads_local, 2, CAP * page_rows, HD)
    cache_rows = cache_rows.transpose(2, 1, 0, 3, 4).reshape(
        2, heads_local, slot_count * page_rows, HD
    )
    key_tags = jnp.repeat(slot_tags, page_rows)
    cached = masked_scores(query_rot, cache_rows[0], segment, key_tags, score_scale)
    row_max = jnp.maximum(jnp.max(local_scores, axis=2), jnp.max(cached, axis=2))
    local_exp = jnp.exp(local_scores - row_max[..., None])
    cached_exp = jnp.exp(cached - row_max[..., None])
    denominator = jnp.sum(local_exp, axis=2) + jnp.sum(cached_exp, axis=2)
    local_weights = (local_exp / denominator[..., None]).astype(jnp.bfloat16)
    cached_weights = (cached_exp / denominator[..., None]).astype(jnp.bfloat16)
    attention = jnp.einsum(
        "hqk,khd->qhd", local_weights, value_heads, preferred_element_type=jnp.float32
    )
    attention = attention + jnp.einsum(
        "hqk,hkd->qhd", cached_weights, cache_rows[1], preferred_element_type=jnp.float32
    )
    attn_flat = attention.astype(jnp.bfloat16).reshape(tok_count, heads_local * HD)
    return project(hidden, spread(attn_flat), gathered, width)


def solution(mesh):
    return jax.shard_map(
        body,
        mesh=mesh,
        in_specs=(
            P("req", "tp"),
            P("req", "tp"),
            P("req", "tp"),
            P("req", "tp"),
            P("req", None, "tp", None),
            P("req", None),
            P("req"),
            P("req", None),
            P(("tp", "req"), None),
            P(("tp", "req"), None),
        ),
        out_specs=P("req", "tp"),
        check_vma=False,
    )
```

time: 221 us -> 198 us (0.90)
  local copies, waits for them, and re-layouts: 31.8 us -> 13.3 us
  Pallas kernels: 166 us -> 177 us
  matrix products: 13 us -> 2.75 us
  other arithmetic: 8.61 us -> 3.89 us
    pallas_call x1, Pallas kernels: 140 us -> 150 us  [exchange(): pl.pallas_call(functools.partial(exchange_kernel, count), out_shape=(jax....]
    dot_general x2 -> x0, matrix products: 9.67 us -> none  [the longest x1 6 us: body(): jnp.dot(mlp_hidden, gathered[:, :, :width].reshape(req_count * shard_rows...]
    slice x2 -> x0, local copies, waits for them, and re-layouts: 9.6 us -> none  [the longest x1 7.83 us: body(): gathered[:, :, :width].reshape(req_count * shard_rows, width)]
    unnamed x23 -> x14, local copies, waits for them, and re-layouts: 4.07 us -> 0.3 us
    pallas_call x1 -> x2, Pallas kernels: 25.9 us -> 27.1 us  [the longest x1 18.3 us: spread(): pl.pallas_call(functools.partial(spread_kernel, groups), out_shape=jax.Sh...]
where the time goes in v2:
time: 198 us
  Pallas kernels  177 us (89%)
  local copies, waits for them, and re-layouts  13.3 us (7%)
  other arithmetic  3.89 us (2%)
  matrix products  2.75 us (1%)
    pallas_call x1, Pallas kernels, exchange(): pl.pallas_call(functools.partial(exchange_kernel, count), out_shape=(jax....  150 us
    pallas_call x1, Pallas kernels, spread(): pl.pallas_call(functools.partial(spread_kernel, groups), out_shape=jax.Sh...  18.3 us
    pallas_call x1, Pallas kernels, project(): pl.pallas_call(functools.partial(project_kernel, fold), out_shape=jax.Sha...  8.79 us
    reshape x2, local copies, waits for them, and re-layouts, body(): send_pages.reshape(req_count, CAP * page_rows, blocks, HD)  6.21 us

profile of v2, /device:TPU:1, one launch (start us, length us, event | category | flops | bytes accessed | tf_op | source)
XLA Modules:
  0.0 197.5 jit_solution(16548299639298925425)
XLA Ops:
  0.0 0.7 fusion.14
  0.8 0.8 select_reduce_fusion.1
  1.7 0.7 multiply_add_fusion
  2.5 0.1 sub.41
  2.6 0.6 pad.4.tags_ref
  3.2 1.8 reshape.208
  5.1 0.8 convolution_convert_fusion
  5.9 2.7 %reshape.209 = bf16[64,32,4,128]{3,2,1,0:T(4,128)(2,1)} reshape(bf16[128,8192]{1,0:T(8,128)(2,1)S(1)} %convolution_convert_fusion) | data formatting | bytes 4194304 | tf_op jit(solution)/shard_map/reshape | solution.py:334
  8.6 3.5 %copy.69 = bf16[64,32,4,128]{3,1,2,0:T(8,128)(2,1)} copy(bf16[64,32,4,128]{3,2,1,0:T(4,128)(2,1)} %reshape.209) | data formatting | bytes 4194304 | tf_op jit(solution)/shard_map/reshape | solution.py:334
  12.2 0.6 copy.46
  12.8 150.3 %exchange.1 = (bf16[8,1024,640]{2,1,0:T(8,128)(2,1)}, bf16[8,128,1024]{2,1,0:T(8,128)(2,1)}, bf16[64,4,32,128]{3,2,1,0:T(8,128)(2,1)}, s32[64,1,128]{2,1,0:T(1,128)}) custom-call(bf16[16,4096]{1,0:T(8,128)(2,1)} %w_ref.1, bf16[8,16,128]{2,1,0:T(8,128)(2,1)} %bitcast.39, bf16[128,1024]{1,0:T(8,128)(2,1)} %h_ref.1, bf16[64,4,32,128]{3,2,1,0:T(8,128)(2,1)} %bitcast.32, ...), custom_call_target="tpu_custom_call" | custom-call | tf_op jit(solution)/shard_map/exchange/pallas_call | solution.py:173
  163.1 1.0 slice_reduce_fusion
  164.1 0.1 eq.107
  164.2 0.1 convert_reduce_fusion.1
  164.3 0.1 convert_reduce_fusion
  164.6 0.1 multiply_cosine_fusion
  164.9 0.1 copy.49
  165.0 0.1 copy.50
  165.2 0.1 copy.54
  165.3 0.1 copy.55
  165.5 0.2 subtract_convert_fusion
  165.9 0.3 fusion.18
  166.3 0.2 broadcast_compare_fusion
  166.6 0.4 copy.68
  167.0 0.4 fusion.17
  167.4 0.7 fusion.19
  168.1 0.4 fusion.1
  168.6 0.8 convolution_bitcast_fusion.1
  169.5 0.2 fusion.4
  169.7 0.7 copy.65.part_ref
  170.5 18.3 %spread.1.a_ref = bf16[8,128,256]{2,1,0:T(8,128)(2,1)} custom-call(bf16[128,256]{1,0:T(8,128)(2,1)} %copy.65.part_ref), custom_call_target="tpu_custom_call" | custom-call | tf_op jit(solution)/shard_map/spread/pallas_call | solution.py:212
  188.7 8.8 %project.1 = bf16[128,512]{1,0:T(8,128)(2,1)} custom-call(bf16[8,128,1024]{2,1,0:T(8,128)(2,1)} %get-tuple-element.9.h_ref, bf16[8,128,256]{2,1,0:T(8,128)(2,1)} %spread.1.a_ref, bf16[8,1024,640]{2,1,0:T(8,128)(2,1)} %get-tuple-element.12.down_ref.proj_ref, bf16[8,1024,640]{2,1,0:T(8,128)(2,1)} %get-tuple-element.12.down_ref.proj_ref), custom_call_target="tpu_custom_call" | custom-call | tf_op jit(solution)/shard_map/project/pallas_call | solution.py:255
  (33 shorter events, 1.2 us)
Async XLA Ops:
  8.6 3.5 %copy-start.4 = (bf16[4,4096]{1,0:T(4,128)(2,1)S(1)}, bf16[4,4096]{1,0:T(4,128)(2,1)}, u32[]{:S(2)}) copy-start(bf16[4,4096]{1,0:T(4,128)(2,1)} %param.18) | copy-start | bytes 98308
  12.1 152.2 %copy-start.5 = (s32[1,128]{1,0:T(1,128)S(1)}, s32[1,128]{1,0:T(1,128)}, u32[]{:S(2)}) copy-start(s32[1,128]{1,0:T(1,128)} %param.17) | copy-start | bytes 1540
  12.1 152.8 %copy-start.1 = (bf16[128,256]{1,0:T(8,128)(2,1)S(1)}, bf16[128,256]{1,0:T(8,128)(2,1)}, u32[]{:S(2)}) copy-start(bf16[128,256]{1,0:T(8,128)(2,1)} %param.10) | copy-start | bytes 196612
  12.1 153.1 %copy-start.2 = (bf16[128,256]{1,0:T(8,128)(2,1)S(1)}, bf16[128,256]{1,0:T(8,128)(2,1)}, u32[]{:S(2)}) copy-start(bf16[128,256]{1,0:T(8,128)(2,1)} %param.11) | copy-start | bytes 196612
  163.1 3.5 %copy-start = (bf16[64,4,32,128]{3,2,1,0:T(8,128)(2,1)S(1)}, bf16[64,4,32,128]{3,2,1,0:T(8,128)(2,1)}, u32[]{:S(2)}) copy-start(bf16[64,4,32,128]{3,2,1,0:T(8,128)(2,1)} %get-tuple-element.11) | copy-start | bytes 6291460
  168.6 0.8 copy-start.3

commit v3 on v2

v3 whole, which is shorter than its diff:
```python
import functools
import math

import jax
import jax.numpy as jnp
from jax import lax
from jax.experimental import pallas as pl
from jax.experimental.pallas import tpu as pltpu
from jax.sharding import PartitionSpec as P

HD = 128
ROT = 32
SEG_DEV = 4
CAP = 2
NX = 4
MESH = pl.DeviceIdType.MESH


def exchange_kernel(count, w_ref, p_ref, h_ref, pages_ref, tags_ref,
                    g_ref, ga_ref, ha_ref, rp_ref, rt_ref,
                    hx_ref, via_ref, vt_ref,
                    send, zr, zl, asend, arecv, psend, precv, tsend, trecv, wsend, wrecv,
                    hsend, hrecv, qsend, qrecv, vsend, vrecv, vtsend, vtrecv):
    me = lax.axis_index("req")
    tp = lax.axis_index("tp")
    groups = ha_ref.shape[0]
    nz = count // NX
    half_z = nz // 2
    x = me // nz
    z = me % nz
    rows, proj = w_ref.shape[0], p_ref.shape[2]
    width = w_ref.shape[1] // groups
    units = h_ref.shape[1] // NX

    def at(dx, dz):
        return ((x + dx + NX) % NX) * nz + (z + dz + nz) % nz

    def span(owner):
        return pl.ds(pl.multiple_of(owner * rows, rows), rows)

    def level(dz):
        return (z + dz + nz) % nz

    barrier = pltpu.get_barrier_semaphore()

    def greet_tp(i, carry):
        pl.semaphore_signal(
            barrier, inc=1, device_id={"tp": (tp + i) % groups}, device_id_type=MESH
        )
        return carry

    def greet(i, carry):
        pl.semaphore_signal(
            barrier, inc=1, device_id={"req": (me + i) % count}, device_id_type=MESH
        )
        return carry

    lax.fori_loop(1, groups, greet_tp, 0)
    lax.fori_loop(1, count, greet, 0)
    pl.semaphore_wait(barrier, count + groups - 2)

    def to_req(src, dst, send_sem, recv_sem, to):
        pltpu.make_async_remote_copy(
            src_ref=src, dst_ref=dst, send_sem=send_sem, recv_sem=recv_sem,
            device_id={"req": to}, device_id_type=MESH,
        ).start()

    def to_tp(src, dst, send_sem, recv_sem, to):
        pltpu.make_async_remote_copy(
            src_ref=src, dst_ref=dst, send_sem=send_sem, recv_sem=recv_sem,
            device_id={"tp": to}, device_id_type=MESH,
        ).start()

    def arrived(ref, sem):
        pltpu.make_async_copy(ref, ref, sem).wait()

    down_slot = g_ref.at[tp, span(z), pl.ds(0, width)]
    proj_slot = g_ref.at[tp, span(z), pl.ds(width, proj)]

    def down_of(g):
        return w_ref.at[:, pl.ds(pl.multiple_of(g * width, width), width)]

    def quarter_of(g):
        return h_ref.at[:, pl.ds(pl.multiple_of(g * units, units), units)]

    def columns_to(i, carry):
        to = (tp + i) % groups
        to_tp(down_of(to), down_slot, wsend.at[0], wrecv.at[0], to)
        to_tp(p_ref.at[to], proj_slot, wsend.at[0], wrecv.at[0], to)
        return carry

    def quarter_to(i, carry):
        to_req(quarter_of((x + i) % NX), hx_ref.at[x], qsend.at[0], qrecv.at[0], at(i, 0))
        return carry

    def hidden_to(i, carry):
        to_tp(hx_ref, ha_ref.at[tp], hsend.at[0], hrecv.at[0], (tp + i) % groups)
        return carry

    def page_to(to):
        to_req(pages_ref.at[to], rp_ref.at[me], psend.at[0], precv.at[0], to)
        to_req(tags_ref.at[to], rt_ref.at[me], tsend.at[0], trecv.at[0], to)

    def pages(dz, first, stop):
        def one(dx, carry):
            page_to(at(dx, dz))
            return carry

        lax.fori_loop(first, stop, one, 0)

    lax.fori_loop(1, groups, columns_to, 0)
    pltpu.make_async_copy(down_of(tp), down_slot, wrecv.at[0]).start()
    pltpu.make_async_copy(p_ref.at[tp], proj_slot, wrecv.at[0]).start()
    lax.fori_loop(1, NX, quarter_to, 0)
    pltpu.make_async_copy(quarter_of(x), hx_ref.at[x], qrecv.at[0]).start()

    hops = half_z // 2
    direct = NX // 2

    def by_stop(dx, carry):
        to = at(dx, -half_z)
        to_req(pages_ref.at[to], via_ref.at[dx - direct], psend.at[0], vrecv.at[0], at(0, -hops))
        to_req(tags_ref.at[to], vt_ref.at[dx - direct], tsend.at[0], vtrecv.at[0], at(0, -hops))
        return carry

    def onward(dx, carry):
        to, source = at(dx, -hops), at(0, hops)
        to_req(via_ref.at[dx - direct], rp_ref.at[source], vsend.at[0], precv.at[0], to)
        to_req(vt_ref.at[dx - direct], rt_ref.at[source], vtsend.at[0], trecv.at[0], to)
        return carry

    pages(half_z, 0, direct)
    lax.fori_loop(direct, NX, by_stop, 0)
    pltpu.make_async_copy(pages_ref.at[me], rp_ref.at[me], precv.at[0]).start()
    pltpu.make_async_copy(tags_ref.at[me], rt_ref.at[me], trecv.at[0]).start()

    right, left = at(0, 1), at(0, -1)

    def across(dz):
        src = g_ref.at[:, span(level(dz)), pl.ds(width, proj)]
        dst = ga_ref.at[:, span(at(0, dz)), :]
        pltpu.make_async_copy(src, dst, arecv.at[0]).start()

        def one(dx, carry):
            to_req(src, dst, asend.at[0], arecv.at[0], at(dx, 0))
            return carry

        lax.fori_loop(1, NX, one, 0)

    def shard(dz):
        return g_ref.at[:, span(level(dz)), :]

    arrived(shard(0), wrecv.at[0])
    to_req(shard(0), shard(0), send.at[0], zr.at[0], right)
    to_req(shard(0), shard(0), send.at[0], zl.at[0], left)
    across(0)
    arrived(hx_ref, qrecv.at[0])
    lax.fori_loop(1, groups, hidden_to, 0)
    pltpu.make_async_copy(hx_ref, ha_ref.at[tp], hrecv.at[0]).start()
    for s in range(1, half_z + 1):
        far = half_z - s
        pages(far, 0 if far else 1, NX)
        if far:
            pages(-far, 0, NX)
        if s == 2:
            arrived(via_ref, vrecv.at[0])
            arrived(vt_ref, vtrecv.at[0])
            lax.fori_loop(direct, NX, onward, 0)
        arrived(shard(-s), zr.at[s - 1])
        if s < half_z:
            to_req(shard(-s), shard(-s), send.at[0], zr.at[s], right)
            arrived(shard(s), zl.at[s - 1])
            if s < half_z - 1:
                to_req(shard(s), shard(s), send.at[0], zl.at[s], left)
            across(s)
        across(-s)
    arrived(ga_ref, arecv.at[0])
    arrived(rp_ref, precv.at[0])
    arrived(rt_ref, trecv.at[0])
    arrived(ha_ref, hrecv.at[0])
    arrived(g_ref.at[:, pl.ds(0, (nz - 1) * rows), :], send.at[0])
    arrived(ga_ref.at[:, pl.ds(0, (NX - 1) * nz * rows), :], asend.at[0])
    arrived(rp_ref.at[pl.ds(0, count - 1)], psend.at[0])
    arrived(rt_ref.at[pl.ds(0, count - 1)], tsend.at[0])
    arrived(via_ref, vsend.at[0])
    arrived(vt_ref, vtsend.at[0])
    arrived(hx_ref.at[pl.ds(0, NX - 1)], qsend.at[0])
    arrived(ha_ref.at[pl.ds(0, groups - 1)], hsend.at[0])
    arrived(g_ref.at[pl.ds(0, groups - 1), pl.ds(0, rows), :], wsend.at[0])


def exchange(down, proj, hidden, send_pages, send_tags):
    count = send_pages.shape[0]
    groups = proj.shape[0]
    nz = count // NX
    any_space = pl.BlockSpec(memory_space=pl.ANY)
    dma = pltpu.SemaphoreType.DMA
    rows, lanes = down.shape[0], proj.shape[2]
    width = down.shape[1] // groups + lanes
    packed = (NX, hidden.shape[0], hidden.shape[1] // NX)
    stops = NX - NX // 2
    return pl.pallas_call(
        functools.partial(exchange_kernel, count),
        out_shape=(
            jax.ShapeDtypeStruct((groups, nz * rows, width), down.dtype),
            jax.ShapeDtypeStruct((groups, count * rows, lanes), down.dtype),
            jax.ShapeDtypeStruct((groups,) + packed, hidden.dtype),
            jax.ShapeDtypeStruct(send_pages.shape, send_pages.dtype),
            jax.ShapeDtypeStruct(send_tags.shape, send_tags.dtype),
        ),
        in_specs=[pl.BlockSpec(memory_space=pltpu.VMEM)] * 5,
        out_specs=(any_space,) * 5,
        scratch_shapes=[
            pltpu.VMEM(packed, hidden.dtype),
            pltpu.VMEM((stops,) + send_pages.shape[1:], send_pages.dtype),
            pltpu.VMEM((stops,) + send_tags.shape[1:], send_tags.dtype),
            dma((1,)), dma((nz // 2,)), dma((nz // 2,)),
        ] + [dma((1,))] * 16,
        compiler_params=pltpu.CompilerParams(collective_id=0, has_side_effects=True),
        name="exchange",
    )(down, proj, hidden, send_pages, send_tags)


def spread_kernel(groups, count, part_ref, quarter_ref, out_ref, quarters_ref,
                  ysend, yrecv, fsend, frecv, qsend, qrecv):
    tp = lax.axis_index("tp")
    me = lax.axis_index("req")
    nz = count // NX
    x, z = me // nz, me % nz
    chips = groups // 2
    other = tp + 1 - 2 * (tp % 2)

    def along(i):
        return (tp + 2 * i) % groups

    def row(i):
        return (x + i) % NX

    barrier = pltpu.get_barrier_semaphore()
    for i in range(1, chips):
        pl.semaphore_signal(barrier, inc=1, device_id={"tp": along(i)}, device_id_type=MESH)
    pl.semaphore_signal(barrier, inc=1, device_id={"tp": other}, device_id_type=MESH)
    for i in range(1, NX):
        pl.semaphore_signal(
            barrier, inc=1, device_id={"req": row(i) * nz + z}, device_id_type=MESH
        )
    pl.semaphore_wait(barrier, chips + NX - 1)

    def copy(src, dst, send_sem, recv_sem, to):
        pltpu.make_async_remote_copy(
            src_ref=src, dst_ref=dst, send_sem=send_sem, recv_sem=recv_sem,
            device_id=to, device_id_type=MESH,
        ).start()

    def arrived(ref, sem):
        pltpu.make_async_copy(ref, ref, sem).wait()

    for i in range(1, chips):
        copy(part_ref, out_ref.at[tp], ysend.at[0], yrecv.at[i - 1], {"tp": along(i)})
    copy(part_ref, out_ref.at[tp], fsend.at[0], frecv.at[0], {"tp": other})
    for i in range(1, NX):
        copy(quarter_ref.at[row(i)], quarters_ref.at[x], qsend.at[0], qrecv.at[0],
             {"req": row(i) * nz + z})
    own = pltpu.make_async_copy(part_ref, out_ref.at[tp], yrecv.at[chips - 1])
    own.start()
    pltpu.make_async_copy(quarter_ref.at[x], quarters_ref.at[x], qrecv.at[0]).start()
    for i in (1, 3, 2):
        block = out_ref.at[along(chips - i)]
        arrived(block, yrecv.at[i - 1])
        copy(block, block, fsend.at[0], frecv.at[0], {"tp": other})
    own.wait()
    arrived(out_ref.at[pl.ds(0, chips)], frecv.at[0])
    arrived(quarters_ref, qrecv.at[0])
    arrived(out_ref.at[pl.ds(0, chips - 1)], ysend.at[0])
    arrived(out_ref.at[pl.ds(0, chips)], fsend.at[0])
    arrived(quarters_ref.at[pl.ds(0, NX - 1)], qsend.at[0])


def spread(part, quarters):
    groups = lax.axis_size("tp")
    vmem = pl.BlockSpec(memory_space=pltpu.VMEM)
    dma = pltpu.SemaphoreType.DMA
    return pl.pallas_call(
        functools.partial(spread_kernel, groups, lax.axis_size("req")),
        out_shape=(
            jax.ShapeDtypeStruct((groups,) + part.shape, part.dtype),
            jax.ShapeDtypeStruct(quarters.shape, quarters.dtype),
        ),
        in_specs=[vmem, vmem],
        out_specs=(vmem, vmem),
        scratch_shapes=[
            dma((1,)), dma((groups // 2,)), dma((1,)), dma((1,)), dma((1,)), dma((1,)),
        ],
        compiler_params=pltpu.CompilerParams(collective_id=1, has_side_effects=True),
        name="spread",
    )(part, quarters)


def down_kernel(h_ref, down_ref, out_ref, total):
    group = pl.program_id(0)
    packs, tokens, units = h_ref.shape[1:]
    hidden = h_ref[0].reshape(packs * tokens, units)
    term = jnp.dot(hidden, down_ref[0], preferred_element_type=jnp.float32)

    @pl.when(group == 0)
    def _():
        total[...] = term

    @pl.when(group > 0)
    def _():
        total[...] += term

    @pl.when(group == pl.num_programs(0) - 1)
    def _():
        out_ref[...] = total[...].reshape(out_ref.shape).astype(out_ref.dtype)


def down_quarters(hidden, gathered, width):
    groups, packs, tokens, units = hidden.shape
    return pl.pallas_call(
        down_kernel,
        out_shape=jax.ShapeDtypeStruct((packs, tokens, width), hidden.dtype),
        grid=(groups,),
        in_specs=[
            pl.BlockSpec((1, packs, tokens, units), lambda g: (g, 0, 0, 0)),
            pl.BlockSpec((1, units, width), lambda g: (g, 0, 0)),
        ],
        out_specs=pl.BlockSpec((packs, tokens, width), lambda g: (0, 0, 0)),
        scratch_shapes=[pltpu.VMEM((packs * tokens, width), jnp.float32)],
        name="down_quarters",
    )(hidden, gathered)


def project_kernel(fold, a_ref, quarters_ref, proj_ref, out_ref, total, wide, flat):
    group = pl.program_id(0)
    lanes = proj_ref.shape[2]
    depth = a_ref.shape[2]
    wide[...] = proj_ref[0].astype(jnp.float32)
    for c in range(fold):
        flat[:, c * lanes:(c + 1) * lanes] = wide[pl.ds(c, depth, stride=fold), :].astype(flat.dtype)
    term = jnp.dot(a_ref[0], flat[...], preferred_element_type=jnp.float32)

    @pl.when(group == 0)
    def _():
        total[...] = term + jnp.sum(quarters_ref[...].astype(jnp.float32), axis=0)

    @pl.when(group > 0)
    def _():
        total[...] += term

    @pl.when(group == pl.num_programs(0) - 1)
    def _():
        out_ref[...] = total[...].astype(out_ref.dtype)


def project(attention, quarters, proj):
    groups, tokens, depth = attention.shape
    width = quarters.shape[2]
    units, lanes = proj.shape[1:]
    return pl.pallas_call(
        functools.partial(project_kernel, width // lanes),
        out_shape=jax.ShapeDtypeStruct((tokens, width), attention.dtype),
        grid=(groups,),
        in_specs=[
            pl.BlockSpec((1, tokens, depth), lambda g: (g, 0, 0)),
            pl.BlockSpec(quarters.shape, lambda g: (0, 0, 0)),
            pl.BlockSpec((1, units, lanes), lambda g: (g, 0, 0)),
        ],
        out_specs=pl.BlockSpec((tokens, width), lambda g: (0, 0)),
        scratch_shapes=[
            pltpu.VMEM((tokens, width), jnp.float32),
            pltpu.VMEM((units, lanes), jnp.float32),
            pltpu.VMEM((depth, width), attention.dtype),
        ],
        name="project",
    )(attention, quarters, proj)


def rotate_heads(values, position, rot_dims):
    half_rot = rot_dims // 2
    frequency = 10000.0 ** (-2.0 * jnp.arange(half_rot, dtype=jnp.float32) / rot_dims)
    angles = position.astype(jnp.float32)[:, None] * frequency[None, :]
    cosine = jnp.cos(angles)[:, None, :]
    sine_part = jnp.sin(angles)[:, None, :]
    leading = values[..., :half_rot]
    trailing = values[..., half_rot:rot_dims]
    return jnp.concatenate(
        [
            leading * cosine - trailing * sine_part,
            trailing * cosine + leading * sine_part,
            values[..., rot_dims:],
        ],
        axis=-1,
    )


def masked_scores(query_rot, block_keys, segment, block_tags, score_scale):
    scores = (
        jnp.einsum("qhd,hkd->hqk", query_rot, block_keys, preferred_element_type=jnp.float32)
        * score_scale
    )
    return jnp.where((segment[:, None] == block_tags[None, :])[None], scores, -jnp.inf)


def body(
    query_new,
    key_new,
    value_new,
    mlp_hidden,
    cache_pages,
    page_dest,
    page_tag,
    seg_ids,
    attn_proj,
    mlp_down,
):
    req_count = lax.axis_size("req")
    tok_count = query_new.shape[0]
    heads_local = query_new.shape[1] // HD
    page_rows = cache_pages.shape[1]
    pages_local = cache_pages.shape[0]
    slot_count = req_count * CAP
    score_scale = 1.0 / math.sqrt(HD)
    destination = page_dest[:, 0]
    dest_match = (destination[:, None] == jnp.arange(req_count, dtype=jnp.int32)[None, :]).astype(
        jnp.int32
    )
    earlier = jnp.cumsum(dest_match, axis=0) - dest_match
    rank = jnp.sum(earlier * dest_match, axis=1)
    slot_of_page = destination * CAP + rank
    select = jnp.arange(slot_count, dtype=jnp.int32)[:, None] == slot_of_page[None, :]
    flat_pages = cache_pages.reshape(pages_local, page_rows * heads_local * 2 * HD)
    send_pages = jnp.dot(
        select.astype(jnp.bfloat16), flat_pages, preferred_element_type=jnp.float32
    ).astype(jnp.bfloat16)
    blocks = 2 * heads_local
    send_pages = (
        send_pages.reshape(req_count, CAP * page_rows, blocks, HD).transpose(0, 2, 1, 3)
    )
    send_tags = (
        jnp.sum(jnp.where(select, page_tag[None, :] + 1, 0), axis=1) - 1
    ).reshape(req_count, 1, CAP)
    send_tags = jnp.pad(send_tags, ((0, 0), (0, 0), (0, HD - CAP)))
    groups = lax.axis_size("tp")
    shard_rows = mlp_down.shape[0]
    proj_rows = attn_proj.shape[0]
    width = mlp_down.shape[1] // groups
    proj = attn_proj.reshape(proj_rows, groups, shard_rows // proj_rows, -1)
    proj = proj.transpose(1, 0, 2, 3).reshape(groups, shard_rows, -1)
    gathered, proj_all, hidden, recv_pages, recv_tags = exchange(
        mlp_down, proj, mlp_hidden, send_pages, send_tags
    )
    slot_tags = recv_tags[:, 0, :CAP].reshape(slot_count)
    segment = seg_ids[0]
    seg_range = jnp.arange(SEG_DEV, dtype=jnp.int32)
    seg_first = jnp.sum((segment[:, None] < seg_range[None, :]).astype(jnp.int32), axis=0)
    prefix = page_rows * jnp.sum(
        (slot_tags[:, None] == seg_range[None, :]).astype(jnp.int32), axis=0
    )
    seg_match = segment[:, None] == seg_range[None, :]
    offset = jnp.sum(jnp.where(seg_match, prefix[None, :] - seg_first[None, :], 0), axis=1)
    row_index = jnp.arange(tok_count, dtype=jnp.int32)
    position = row_index + offset
    query_rot = rotate_heads(
        query_new.reshape(tok_count, heads_local, HD).astype(jnp.float32), position, ROT
    ).astype(jnp.bfloat16)
    key_rot = rotate_heads(
        key_new.reshape(tok_count, heads_local, HD).astype(jnp.float32), position, ROT
    ).astype(jnp.bfloat16)
    value_heads = value_new.reshape(tok_count, heads_local, HD)
    local_scores = (
        jnp.einsum("qhd,khd->hqk", query_rot, key_rot, preferred_element_type=jnp.float32)
        * score_scale
    )
    causal = (segment[:, None] == segment[None, :]) & (row_index[None, :] <= row_index[:, None])
    local_scores = jnp.where(causal[None], local_scores, -jnp.inf)
    cache_rows = recv_pages.reshape(req_count, heads_local, 2, CAP * page_rows, HD)
    cache_rows = cache_rows.transpose(2, 1, 0, 3, 4).reshape(
        2, heads_local, slot_count * page_rows, HD
    )
    key_tags = jnp.repeat(slot_tags, page_rows)
    cached = masked_scores(query_rot, cache_rows[0], segment, key_tags, score_scale)
    row_max = jnp.maximum(jnp.max(local_scores, axis=2), jnp.max(cached, axis=2))
    local_exp = jnp.exp(local_scores - row_max[..., None])
    cached_exp = jnp.exp(cached - row_max[..., None])
    denominator = jnp.sum(local_exp, axis=2) + jnp.sum(cached_exp, axis=2)
    local_weights = (local_exp / denominator[..., None]).astype(jnp.bfloat16)
    cached_weights = (cached_exp / denominator[..., None]).astype(jnp.bfloat16)
    attention = jnp.einsum(
        "hqk,khd->qhd", local_weights, value_heads, preferred_element_type=jnp.float32
    )
    attention = attention + jnp.einsum(
        "hqk,hkd->qhd", cached_weights, cache_rows[1], preferred_element_type=jnp.float32
    )
    attn_flat = attention.astype(jnp.bfloat16).reshape(tok_count, heads_local * HD)
    attention_all, quarters = spread(attn_flat, down_quarters(hidden, gathered, width))
    return project(attention_all, quarters, proj_all)


def solution(mesh):
    return jax.shard_map(
        body,
        mesh=mesh,
        in_specs=(
            P("req", "tp"),
            P("req", "tp"),
            P("req", "tp"),
            P("req", "tp"),
            P("req", None, "tp", None),
            P("req", None),
            P("req"),
            P("req", None),
            P(("tp", "req"), None),
            P(("tp", "req"), None),
        ),
        out_specs=P("req", "tp"),
        check_vma=False,
    )
```

time: 198 us -> 205 us (1.035)
  local copies, waits for them, and re-layouts: 13.3 us -> 18.3 us
  other arithmetic: 3.89 us -> 6.38 us
    unnamed x14, local copies, waits for them, and re-layouts: 0.3 us -> 2.52 us
    pallas_call x2 -> x3, Pallas kernels: 27.1 us -> 28 us  [the longest x1 14.5 us: spread(): pl.pallas_call(functools.partial(spread_kernel, groups, lax.axis_size('re...]
where the time goes in v3:
time: 205 us
  Pallas kernels  176 us (86%)
  local copies, waits for them, and re-layouts  18.3 us (9%)
  other arithmetic  6.38 us (3%)
  matrix products  3.34 us (2%)
    pallas_call x1, Pallas kernels, exchange(): pl.pallas_call(functools.partial(exchange_kernel, count), out_shape=(jax....  148 us
    pallas_call x1, Pallas kernels, spread(): pl.pallas_call(functools.partial(spread_kernel, groups, lax.axis_size('re...  14.5 us
    pallas_call x1, Pallas kernels, down_quarters(): pl.pallas_call(down_kernel, out_shape=jax.ShapeDtypeStruct((packs, tokens...  7.08 us
    pallas_call x1, Pallas kernels, project(): pl.pallas_call(functools.partial(project_kernel, width // lanes), out_sha...  6.45 us
    reshape x2, local copies, waits for them, and re-layouts, body(): send_pages.reshape(req_count, CAP * page_rows, blocks, HD)  6.3 us

profile of v3, /device:TPU:1, one launch (start us, length us, event | category | flops | bytes accessed | tf_op | source)
XLA Modules:
  0.0 204.6 jit_solution(13354189958961279050)
XLA Ops:
  0.0 1.4 convert_reduce_fusion
  1.4 0.5 multiply_power_fusion
  1.9 0.8 fusion.13
  2.7 0.8 reshape.206
  3.5 0.6 copy.48
  4.2 0.7 fusion.14
  5.0 0.8 select_reduce_fusion.1
  5.8 0.7 multiply_add_fusion
  6.6 0.4 copy-done.3
  7.2 0.6 pad.4.tags_ref
  7.8 0.9 copy.46
  9.0 1.0 copy.54
  10.2 1.6 copy.64
  11.8 0.8 reshape.208
  12.6 1.4 convolution_convert_fusion
  14.1 2.7 %reshape.209 = bf16[64,32,4,128]{3,2,1,0:T(4,128)(2,1)} reshape(bf16[128,8192]{1,0:T(8,128)(2,1)S(1)} %convolution_convert_fusion) | data formatting | bytes 4194304 | tf_op jit(solution)/shard_map/reshape | solution.py:438
  16.8 3.6 %copy.69 = bf16[64,32,4,128]{3,1,2,0:T(8,128)(2,1)} copy(bf16[64,32,4,128]{3,2,1,0:T(4,128)(2,1)} %reshape.209) | data formatting | bytes 4194304 | tf_op jit(solution)/shard_map/reshape | solution.py:438
  20.4 148.3 %exchange.1 = (bf16[8,256,640]{2,1,0:T(8,128)(2,1)}, bf16[8,1024,128]{2,1,0:T(8,128)(2,1)}, bf16[8,4,128,256]{3,2,1,0:T(8,128)(2,1)}, bf16[64,4,32,128]{3,2,1,0:T(8,128)(2,1)}, s32[64,1,128]{2,1,0:T(1,128)}) custom-call(bf16[16,4096]{1,0:T(8,128)(2,1)} %w_ref.1, bf16[8,16,128]{2,1,0:T(8,128)(2,1)} %bitcast.39, bf16[128,1024]{1,0:T(8,128)(2,1)} %h_ref.1, ...), custom_call_target="tpu_custom_call" | custom-call | tf_op jit(solution)/shard_map/exchange/pallas_call | solution.py:202
  168.7 0.8 slice_reduce_fusion
  169.7 2.0 copy.68
  171.7 0.4 fusion.17
  172.9 0.1 subtract_convert_fusion
  173.1 0.3 fusion.18
  173.4 0.2 broadcast_compare_fusion
  173.6 7.1 %down_quarters.1.quarter_ref = bf16[4,128,512]{2,1,0:T(8,128)(2,1)} custom-call(bf16[8,4,128,256]{3,2,1,0:T(8,128)(2,1)} %get-tuple-element.14.h_ref, bf16[8,256,640]{2,1,0:T(8,128)(2,1)} %get-tuple-element.15.down_ref), custom_call_target="tpu_custom_call" | custom-call | tf_op jit(solution)/shard_map/down_quarters/pallas_call | solution.py:320
  180.7 0.7 fusion.19
  181.4 0.4 fusion.1
  181.9 0.8 convolution_bitcast_fusion.1
  182.7 0.2 fusion.4
  182.9 0.7 copy.65.part_ref
  183.6 14.5 %spread.1 = (bf16[8,128,256]{2,1,0:T(8,128)(2,1)}, bf16[4,128,512]{2,1,0:T(8,128)(2,1)}) custom-call(bf16[128,256]{1,0:T(8,128)(2,1)} %copy.65.part_ref, bf16[4,128,512]{2,1,0:T(8,128)(2,1)} %down_quarters.1.quarter_ref), custom_call_target="tpu_custom_call" | custom-call | tf_op jit(solution)/shard_map/spread/pallas_call | solution.py:283
  198.1 6.4 %project.1 = bf16[128,512]{1,0:T(8,128)(2,1)} custom-call(bf16[8,128,256]{2,1,0:T(8,128)(2,1)} %get-tuple-element.16.a_ref, bf16[4,128,512]{2,1,0:T(8,128)(2,1)} %get-tuple-element.17.quarters_ref, bf16[8,1024,128]{2,1,0:T(8,128)(2,1)} %get-tuple-element.18.proj_ref), custom_call_target="tpu_custom_call" | custom-call | tf_op jit(solution)/shard_map/project/pallas_call | solution.py:360
  (34 shorter events, 1.8 us)
Async XLA Ops:
  0.0 11.8 %copy-start = (bf16[64,16,2,256]{3,2,1,0:T(2,128)(2,1)S(1)}, bf16[64,16,2,256]{3,2,1,0:T(2,128)(2,1)}, u32[]{:S(2)}) copy-start(bf16[64,16,2,256]{3,2,1,0:T(2,128)(2,1)} %param.14) | copy-start | bytes 3145732
  6.5 0.5 copy-start.3
  171.7 0.6 copy-start.5
  171.7 0.7 copy-start.2
  171.7 0.7 copy-start.4
  181.9 0.8 copy-start.1

commit v4 on v2

--- a/solution.py
+++ b/solution.py
@@ -17,8 +17,8 @@
 
 
 def exchange_kernel(count, w_ref, p_ref, h_ref, pages_ref, tags_ref, g_ref, ha_ref, rp_ref, rt_ref,
-                    send, zr, zl, xp, xm, relay, psend, precv, tsend, trecv, wsend, wrecv,
-                    hsend, hrecv):
+                    via_ref, vt_ref, send, zr, zl, xp, xm, relay, psend, precv, tsend, trecv, wsend, wrecv,
+                    hsend, hrecv, vsend, vrecv, vtsend, vtrecv):
     me = lax.axis_index("req")
     tp = lax.axis_index("tp")
     groups = ha_ref.shape[0]
@@ -88,25 +88,41 @@
         ).start()
         return carry
 
-    def pages(dz, first):
+    def to_req(src, dst, send_sem, recv_sem, to):
+        pltpu.make_async_remote_copy(
+            src_ref=src, dst_ref=dst, send_sem=send_sem, recv_sem=recv_sem,
+            device_id={"req": to}, device_id_type=MESH,
+        ).start()
+
+    def pages(dz, first, stop=NX):
         def one(dx, carry):
             to = at(dx, dz)
-            pltpu.make_async_remote_copy(
-                src_ref=pages_ref.at[to], dst_ref=rp_ref.at[me], send_sem=psend.at[0],
-                recv_sem=precv.at[0], device_id={"req": to}, device_id_type=MESH,
-            ).start()
-            pltpu.make_async_remote_copy(
-                src_ref=tags_ref.at[to], dst_ref=rt_ref.at[me], send_sem=tsend.at[0],
-                recv_sem=trecv.at[0], device_id={"req": to}, device_id_type=MESH,
-            ).start()
+            to_req(pages_ref.at[to], rp_ref.at[me], psend.at[0], precv.at[0], to)
+            to_req(tags_ref.at[to], rt_ref.at[me], tsend.at[0], trecv.at[0], to)
             return carry
 
-        lax.fori_loop(first, NX, one, 0)
+        lax.fori_loop(first, stop, one, 0)
+
+    hops = half_z // 2
+    direct = NX // 2
+
+    def by_stop(dx, carry):
+        to = at(dx, -half_z)
+        to_req(pages_ref.at[to], via_ref.at[dx - direct], psend.at[0], vrecv.at[0], at(0, -hops))
+        to_req(tags_ref.at[to], vt_ref.at[dx - direct], tsend.at[0], vtrecv.at[0], at(0, -hops))
+        return carry
+
+    def onward(dx, carry):
+        to, source = at(dx, -hops), at(0, hops)
+        to_req(via_ref.at[dx - direct], rp_ref.at[source], vsend.at[0], precv.at[0], to)
+        to_req(vt_ref.at[dx - direct], rt_ref.at[source], vtsend.at[0], trecv.at[0], to)
+        return carry
 
     lax.fori_loop(1, groups, columns_to, 0)
     pltpu.make_async_copy(down_of(tp), down_slot, wrecv.at[0]).start()
     pltpu.make_async_copy(p_ref.at[tp], proj_slot, wrecv.at[0]).start()
     pages(0, 1)
+    lax.fori_loop(direct, NX, by_stop, 0)
     lax.fori_loop(1, groups, hidden_to, 0)
     pltpu.make_async_copy(h_ref, ha_ref.at[tp], hrecv.at[0]).start()
     pltpu.make_async_copy(pages_ref.at[me], rp_ref.at[me], precv.at[0]).start()
@@ -142,9 +158,13 @@
                 push(above, zl.at[s], left)
             push(above, xp.at[2 * s], plus)
             push(above, xm.at[2 * s], minus)
-        pages(s, 0)
+        pages(s, 0, NX if s < half_z else direct)
         if s < half_z:
             pages(-s, 0)
+        if s == 2:
+            arrived(via_ref, vrecv.at[0])
+            arrived(vt_ref, vtrecv.at[0])
+            lax.fori_loop(direct, NX, onward, 0)
         if s == 1:
             relays(0, 0)
         else:
@@ -158,6 +178,8 @@
     arrived(ha_ref, hrecv.at[0])
     arrived(rp_ref.at[pl.ds(0, count - 1)], psend.at[0])
     arrived(rt_ref.at[pl.ds(0, count - 1)], tsend.at[0])
+    arrived(via_ref, vsend.at[0])
+    arrived(vt_ref, vtsend.at[0])
     arrived(ha_ref.at[pl.ds(0, groups - 1)], hsend.at[0])
     arrived(g_ref.at[pl.ds(0, groups - 1), pl.ds(0, rows), :], wsend.at[0])
 
@@ -181,95 +203,90 @@
         in_specs=[pl.BlockSpec(memory_space=pltpu.VMEM)] * 5,
         out_specs=(any_space,) * 4,
         scratch_shapes=[
+            pltpu.VMEM((NX - NX // 2,) + send_pages.shape[1:], send_pages.dtype),
+            pltpu.VMEM((NX - NX // 2,) + send_tags.shape[1:], send_tags.dtype),
             dma((1,)), dma((half_z,)), dma((half_z,)), dma((2 * half_z,)), dma((2 * half_z,)),
-        ] + [dma((1,))] * 9,
+        ] + [dma((1,))] * 13,
         compiler_params=pltpu.CompilerParams(collective_id=0, has_side_effects=True),
         name="exchange",
     )(down, proj, hidden, send_pages, send_tags)
 
 
-def spread_kernel(groups, part_ref, out_ref, send, recv):
+def project_kernel(groups, part_ref, h_ref, g_ref, out_ref,
+                   all_ref, hid, wts, total, wide, flat, send, recv, hsem, gsem):
     me = lax.axis_index("tp")
+    width = out_ref.shape[1]
+    lanes = g_ref.shape[2] - width
+    depth = part_ref.shape[1]
+
+    def load(g, carry):
+        pltpu.make_async_copy(h_ref.at[g], hid.at[g], hsem.at[g]).start()
+        pltpu.make_async_copy(g_ref.at[g], wts.at[g], gsem.at[g]).start()
+        return carry
+
     barrier = pltpu.get_barrier_semaphore()
     for i in range(1, groups):
         pl.semaphore_signal(
             barrier, inc=1, device_id={"tp": (me + i) % groups}, device_id_type=MESH
         )
+    lax.fori_loop(0, groups, load, 0)
     pl.semaphore_wait(barrier, groups - 1)
     for i in range(1, groups):
         pltpu.make_async_remote_copy(
-            src_ref=part_ref, dst_ref=out_ref.at[me], send_sem=send, recv_sem=recv,
+            src_ref=part_ref, dst_ref=all_ref.at[me], send_sem=send.at[0], recv_sem=recv.at[0],
             device_id={"tp": (me + i) % groups}, device_id_type=MESH,
         ).start()
-    pltpu.make_async_copy(part_ref, out_ref.at[me], recv).start()
-    pltpu.make_async_copy(out_ref, out_ref, recv).wait()
-    rest = out_ref.at[pl.ds(0, groups - 1)]
-    pltpu.make_async_copy(rest, rest, send).wait()
-
-
-def spread(part):
-    groups = lax.axis_size("tp")
+    pltpu.make_async_copy(part_ref, all_ref.at[me], recv.at[0]).start()
+    total[...] = jnp.zeros_like(total)
+
+    def local_term(g, carry):
+        pltpu.make_async_copy(h_ref.at[g], hid.at[g], hsem.at[g]).wait()
+        pltpu.make_async_copy(g_ref.at[g], wts.at[g], gsem.at[g]).wait()
+        total[...] += jnp.dot(hid[g], wts[g, :, :width], preferred_element_type=jnp.float32)
+        wide[...] = wts[g, :, width:].astype(jnp.float32)
+        for c in range(width // lanes):
+            flat[g, :, c * lanes:(c + 1) * lanes] = wide[
+                pl.ds(c, depth, stride=width // lanes), :
+            ].astype(flat.dtype)
+        return carry
+
+    lax.fori_loop(0, groups, local_term, 0)
+    pltpu.make_async_copy(all_ref, all_ref, recv.at[0]).wait()
+
+    def spread_term(g, carry):
+        total[...] += jnp.dot(all_ref[g], flat[g], preferred_element_type=jnp.float32)
+        return carry
+
+    lax.fori_loop(0, groups, spread_term, 0)
+    out_ref[...] = total[...].astype(out_ref.dtype)
+    rest = all_ref.at[pl.ds(0, groups - 1)]
+    pltpu.make_async_copy(rest, rest, send.at[0]).wait()
+
+
+def project(part, hidden, gathered, width):
+    groups, units = gathered.shape[:2]
+    tokens, depth = part.shape
+    lanes = gathered.shape[2] - width
+    vmem = pl.BlockSpec(memory_space=pltpu.VMEM)
+    any_space = pl.BlockSpec(memory_space=pl.ANY)
+    dma = pltpu.SemaphoreType.DMA
     return pl.pallas_call(
-        functools.partial(spread_kernel, groups),
-        out_shape=jax.ShapeDtypeStruct((groups,) + part.shape, part.dtype),
-        in_specs=[pl.BlockSpec(memory_space=pltpu.VMEM)],
-        out_specs=pl.BlockSpec(memory_space=pltpu.VMEM),
-        scratch_shapes=[pltpu.SemaphoreType.DMA, pltpu.SemaphoreType.DMA],
-        compiler_params=pltpu.CompilerParams(collective_id=1, has_side_effects=True),
-        name="spread",
-    )(part)
-
-
-def project_kernel(fold, h_ref, a_ref, down_ref, proj_ref, out_ref, total, wide, flat):
-    group = pl.program_id(0)
-    lanes = proj_ref.shape[2]
-    depth = a_ref.shape[2]
-    wide[...] = proj_ref[0].astype(jnp.float32)
-    for c in range(fold):
-        flat[:, c * lanes:(c + 1) * lanes] = wide[pl.ds(c, depth, stride=fold), :].astype(flat.dtype)
-    term = jnp.dot(h_ref[0], down_ref[0], preferred_element_type=jnp.float32)
-    term = term + jnp.dot(a_ref[0], flat[...], preferred_element_type=jnp.float32)
-
-    @pl.when(group == 0)
-    def _():
-        total[...] = term
-
-    @pl.when(group > 0)
-    def _():
-        total[...] += term
-
-    @pl.when(group == pl.num_programs(0) - 1)
-    def _():
-        out_ref[...] = total[...].astype(out_ref.dtype)
-
-
-def project(hidden, attention, gathered, width):
-    groups, tokens, units = hidden.shape
-    depth = attention.shape[2]
-    lanes = gathered.shape[2] - width
-    fold = width // lanes
-
-    def block(rows, columns, at=0):
-        return pl.BlockSpec((1, rows, columns), lambda g: (g, 0, at))
-
-    return pl.pallas_call(
-        functools.partial(project_kernel, fold),
-        out_shape=jax.ShapeDtypeStruct((tokens, width), hidden.dtype),
-        grid=(groups,),
-        in_specs=[
-            block(tokens, units),
-            block(tokens, depth),
-            block(units, width),
-            block(units, lanes, fold),
-        ],
-        out_specs=pl.BlockSpec((tokens, width), lambda g: (0, 0)),
+        functools.partial(project_kernel, groups),
+        out_shape=jax.ShapeDtypeStruct((tokens, width), part.dtype),
+        in_specs=[vmem, any_space, any_space],
+        out_specs=vmem,
         scratch_shapes=[
+            pltpu.VMEM((groups,) + part.shape, part.dtype),
+            pltpu.VMEM(hidden.shape, hidden.dtype),
+            pltpu.VMEM(gathered.shape, gathered.dtype),
             pltpu.VMEM((tokens, width), jnp.float32),
             pltpu.VMEM((units, lanes), jnp.float32),
-            pltpu.VMEM((depth, width), hidden.dtype),
+            pltpu.VMEM((groups, depth, width), part.dtype),
+            dma((1,)), dma((1,)), dma((groups,)), dma((groups,)),
         ],
+        compiler_params=pltpu.CompilerParams(collective_id=1, has_side_effects=True),
         name="project",
-    )(hidden, attention, gathered, gathered)
+    )(part, hidden, gathered)
 
 
 def rotate_heads(values, position, rot_dims):
@@ -389,7 +406,7 @@
         "hqk,hkd->qhd", cached_weights, cache_rows[1], preferred_element_type=jnp.float32
     )
     attn_flat = attention.astype(jnp.bfloat16).reshape(tok_count, heads_local * HD)
-    return project(hidden, spread(attn_flat), gathered, width)
+    return project(attn_flat, hidden, gathered, width)
 
 
 def solution(mesh):

time: 198 us -> 186 us (0.939)
  Pallas kernels: 177 us -> 163 us
    pallas_call x1, Pallas kernels: 150 us -> 142 us  [exchange(): pl.pallas_call(functools.partial(exchange_kernel, count), out_shape=(jax....]
    pallas_call x2 -> x1, Pallas kernels: 27.1 us -> 21.1 us  [project(): pl.pallas_call(functools.partial(project_kernel, groups), out_shape=jax.S...]
where the time goes in v4:
time: 186 us; the launch traced here: 185 us
  Pallas kernels  163 us (88%)
  local copies, waits for them, and re-layouts  14.9 us (8%)
  other arithmetic  3.89 us (2%)
  matrix products  2.73 us (1%)
    pallas_call x1, Pallas kernels, exchange(): pl.pallas_call(functools.partial(exchange_kernel, count), out_shape=(jax....  142 us
    pallas_call x1, Pallas kernels, project(): pl.pallas_call(functools.partial(project_kernel, groups), out_shape=jax.S...  21.1 us
    reshape x2, local copies, waits for them, and re-layouts, body(): send_pages.reshape(req_count, CAP * page_rows, blocks, HD)  6.21 us

profile of v4, /device:TPU:1, one launch (start us, length us, event | category | flops | bytes accessed | tf_op | source)
XLA Modules:
  0.0 185.2 jit_solution(849629075503083646)
XLA Ops:
  0.0 0.7 fusion.14
  0.8 0.8 select_reduce_fusion.1
  1.7 0.7 multiply_add_fusion
  2.5 0.1 sub.41
  2.6 0.6 pad.4.tags_ref
  3.2 1.8 reshape.208
  5.1 0.8 convolution_convert_fusion
  5.9 2.7 %reshape.209 = bf16[64,32,4,128]{3,2,1,0:T(4,128)(2,1)} reshape(bf16[128,8192]{1,0:T(8,128)(2,1)S(1)} %convolution_convert_fusion) | data formatting | bytes 4194304 | tf_op jit(solution)/shard_map/reshape | solution.py:351
  8.6 3.5 %copy.69 = bf16[64,32,4,128]{3,1,2,0:T(8,128)(2,1)} copy(bf16[64,32,4,128]{3,2,1,0:T(4,128)(2,1)} %reshape.209) | data formatting | bytes 4194304 | tf_op jit(solution)/shard_map/reshape | solution.py:351
  12.2 0.6 copy.48
  12.8 142.3 %exchange.1 = (bf16[8,1024,640]{2,1,0:T(8,128)(2,1)}, bf16[8,128,1024]{2,1,0:T(8,128)(2,1)}, bf16[64,4,32,128]{3,2,1,0:T(8,128)(2,1)}, s32[64,1,128]{2,1,0:T(1,128)}) custom-call(bf16[16,4096]{1,0:T(8,128)(2,1)} %w_ref.1, bf16[8,16,128]{2,1,0:T(8,128)(2,1)} %bitcast.39, bf16[128,1024]{1,0:T(8,128)(2,1)} %h_ref.1, bf16[64,4,32,128]{3,2,1,0:T(8,128)(2,1)} %bitcast.32, ...), custom_call_target="tpu_custom_call" | custom-call | tf_op jit(solution)/shard_map/exchange/pallas_call | solution.py:195
  155.1 1.0 slice_reduce_fusion
  156.1 0.1 eq.107
  156.2 0.1 convert_reduce_fusion.1
  156.4 0.1 convert_reduce_fusion
  156.6 0.1 multiply_cosine_fusion
  156.9 0.1 copy.46
  157.1 0.1 copy.47
  157.2 0.1 copy.54
  157.3 0.1 copy.55
  157.5 0.2 subtract_convert_fusion
  157.9 0.3 fusion.18
  158.4 0.2 broadcast_compare_fusion
  158.6 0.4 copy.68
  159.0 0.4 fusion.17
  159.5 0.7 fusion.19
  160.2 0.4 fusion.1
  160.7 0.8 convolution_bitcast_fusion.1
  161.6 0.2 fusion.4
  161.8 0.7 copy.65.part_ref
  162.5 21.1 %project.1 = bf16[128,512]{1,0:T(8,128)(2,1)} custom-call(bf16[128,256]{1,0:T(8,128)(2,1)} %copy.65.part_ref, bf16[8,128,1024]{2,1,0:T(8,128)(2,1)} %get-tuple-element.11.h_ref, bf16[8,1024,640]{2,1,0:T(8,128)(2,1)} %get-tuple-element.12.g_ref), custom_call_target="tpu_custom_call" | custom-call | tf_op jit(solution)/shard_map/project/pallas_call | solution.py:273
  183.7 1.6 copy.71
  (33 shorter events, 1.2 us)
Async XLA Ops:
  8.6 3.5 %copy-start.4 = (bf16[4,4096]{1,0:T(4,128)(2,1)S(1)}, bf16[4,4096]{1,0:T(4,128)(2,1)}, u32[]{:S(2)}) copy-start(bf16[4,4096]{1,0:T(4,128)(2,1)} %param.18) | copy-start | bytes 98308
  12.1 144.3 %copy-start.5 = (s32[1,128]{1,0:T(1,128)S(1)}, s32[1,128]{1,0:T(1,128)}, u32[]{:S(2)}) copy-start(s32[1,128]{1,0:T(1,128)} %param.17) | copy-start | bytes 1540
  12.1 144.8 %copy-start.1 = (bf16[128,256]{1,0:T(8,128)(2,1)S(1)}, bf16[128,256]{1,0:T(8,128)(2,1)}, u32[]{:S(2)}) copy-start(bf16[128,256]{1,0:T(8,128)(2,1)} %param.10) | copy-start | bytes 196612
  12.1 145.1 %copy-start.2 = (bf16[128,256]{1,0:T(8,128)(2,1)S(1)}, bf16[128,256]{1,0:T(8,128)(2,1)}, u32[]{:S(2)}) copy-start(bf16[128,256]{1,0:T(8,128)(2,1)} %param.11) | copy-start | bytes 196612
  155.1 3.5 %copy-start = (bf16[64,4,32,128]{3,2,1,0:T(8,128)(2,1)S(1)}, bf16[64,4,32,128]{3,2,1,0:T(8,128)(2,1)}, u32[]{:S(2)}) copy-start(bf16[64,4,32,128]{3,2,1,0:T(8,128)(2,1)} %get-tuple-element.10) | copy-start | bytes 6291460
  160.7 0.8 copy-start.3

commit v5 on v4

--- a/solution.py
+++ b/solution.py
@@ -121,7 +121,7 @@
     lax.fori_loop(1, groups, columns_to, 0)
     pltpu.make_async_copy(down_of(tp), down_slot, wrecv.at[0]).start()
     pltpu.make_async_copy(p_ref.at[tp], proj_slot, wrecv.at[0]).start()
-    pages(0, 1)
+    pages(half_z, 0, direct)
     lax.fori_loop(direct, NX, by_stop, 0)
     lax.fori_loop(1, groups, hidden_to, 0)
     pltpu.make_async_copy(h_ref, ha_ref.at[tp], hrecv.at[0]).start()
@@ -158,9 +158,10 @@
                 push(above, zl.at[s], left)
             push(above, xp.at[2 * s], plus)
             push(above, xm.at[2 * s], minus)
-        pages(s, 0, NX if s < half_z else direct)
-        if s < half_z:
-            pages(-s, 0)
+        far = half_z - s
+        pages(far, 0 if far else 1)
+        if far:
+            pages(-far, 0)
         if s == 2:
             arrived(via_ref, vrecv.at[0])
             arrived(vt_ref, vtrecv.at[0])

time: 186 us -> 199 us (1.070)
  Pallas kernels: 163 us -> 177 us
    pallas_call x1, Pallas kernels: 142 us -> 161 us  [exchange(): pl.pallas_call(functools.partial(exchange_kernel, count), out_shape=(jax....]
    pallas_call x1, Pallas kernels: 21.1 us -> 15.4 us  [project(): pl.pallas_call(functools.partial(project_kernel, groups), out_shape=jax.S...]
where the time goes in v5:
time: 199 us
  Pallas kernels  177 us (89%)
  local copies, waits for them, and re-layouts  14.9 us (7%)
  other arithmetic  3.89 us (2%)
  matrix products  2.73 us (1%)
    pallas_call x1, Pallas kernels, exchange(): pl.pallas_call(functools.partial(exchange_kernel, count), out_shape=(jax....  161 us
    pallas_call x1, Pallas kernels, project(): pl.pallas_call(functools.partial(project_kernel, groups), out_shape=jax.S...  15.4 us
    reshape x2, local copies, waits for them, and re-layouts, body(): send_pages.reshape(req_count, CAP * page_rows, blocks, HD)  6.21 us

profile of v5, /device:TPU:1, one launch (start us, length us, event | category | flops | bytes accessed | tf_op | source)
XLA Modules:
  0.0 198.5 jit_solution(8694739249950702504)
XLA Ops:
  0.0 0.7 fusion.14
  0.8 0.8 select_reduce_fusion.1
  1.7 0.7 multiply_add_fusion
  2.5 0.1 sub.41
  2.6 0.6 pad.4.tags_ref
  3.2 1.8 reshape.208
  5.1 0.8 convolution_convert_fusion
  5.9 2.7 %reshape.209 = bf16[64,32,4,128]{3,2,1,0:T(4,128)(2,1)} reshape(bf16[128,8192]{1,0:T(8,128)(2,1)S(1)} %convolution_convert_fusion) | data formatting | bytes 4194304 | tf_op jit(solution)/shard_map/reshape | solution.py:352
  8.6 3.5 %copy.69 = bf16[64,32,4,128]{3,1,2,0:T(8,128)(2,1)} copy(bf16[64,32,4,128]{3,2,1,0:T(4,128)(2,1)} %reshape.209) | data formatting | bytes 4194304 | tf_op jit(solution)/shard_map/reshape | solution.py:352
  12.2 0.6 copy.48
  12.8 161.3 %exchange.1 = (bf16[8,1024,640]{2,1,0:T(8,128)(2,1)}, bf16[8,128,1024]{2,1,0:T(8,128)(2,1)}, bf16[64,4,32,128]{3,2,1,0:T(8,128)(2,1)}, s32[64,1,128]{2,1,0:T(1,128)}) custom-call(bf16[16,4096]{1,0:T(8,128)(2,1)} %w_ref.1, bf16[8,16,128]{2,1,0:T(8,128)(2,1)} %bitcast.39, bf16[128,1024]{1,0:T(8,128)(2,1)} %h_ref.1, bf16[64,4,32,128]{3,2,1,0:T(8,128)(2,1)} %bitcast.32, ...), custom_call_target="tpu_custom_call" | custom-call | tf_op jit(solution)/shard_map/exchange/pallas_call | solution.py:196
  174.1 1.0 slice_reduce_fusion
  175.1 0.1 eq.107
  175.3 0.1 convert_reduce_fusion.1
  175.4 0.1 convert_reduce_fusion
  175.6 0.1 multiply_cosine_fusion
  175.9 0.1 copy.46
  176.1 0.1 copy.47
  176.2 0.1 copy.54
  176.3 0.1 copy.55
  176.5 0.2 subtract_convert_fusion
  176.9 0.3 fusion.18
  177.4 0.2 broadcast_compare_fusion
  177.6 0.4 copy.68
  178.0 0.4 fusion.17
  178.5 0.7 fusion.19
  179.2 0.4 fusion.1
  179.7 0.8 convolution_bitcast_fusion.1
  180.6 0.2 fusion.4
  180.8 0.7 copy.65.part_ref
  181.6 15.4 %project.1 = bf16[128,512]{1,0:T(8,128)(2,1)} custom-call(bf16[128,256]{1,0:T(8,128)(2,1)} %copy.65.part_ref, bf16[8,128,1024]{2,1,0:T(8,128)(2,1)} %get-tuple-element.11.h_ref, bf16[8,1024,640]{2,1,0:T(8,128)(2,1)} %get-tuple-element.12.g_ref), custom_call_target="tpu_custom_call" | custom-call | tf_op jit(solution)/shard_map/project/pallas_call | solution.py:274
  196.9 1.6 copy.71
  (33 shorter events, 1.2 us)
Async XLA Ops:
  8.6 3.5 %copy-start.4 = (bf16[4,4096]{1,0:T(4,128)(2,1)S(1)}, bf16[4,4096]{1,0:T(4,128)(2,1)}, u32[]{:S(2)}) copy-start(bf16[4,4096]{1,0:T(4,128)(2,1)} %param.18) | copy-start | bytes 98308
  12.1 163.3 %copy-start.5 = (s32[1,128]{1,0:T(1,128)S(1)}, s32[1,128]{1,0:T(1,128)}, u32[]{:S(2)}) copy-start(s32[1,128]{1,0:T(1,128)} %param.17) | copy-start | bytes 1540
  12.1 163.8 %copy-start.1 = (bf16[128,256]{1,0:T(8,128)(2,1)S(1)}, bf16[128,256]{1,0:T(8,128)(2,1)}, u32[]{:S(2)}) copy-start(bf16[128,256]{1,0:T(8,128)(2,1)} %param.10) | copy-start | bytes 196612
  12.1 164.1 %copy-start.2 = (bf16[128,256]{1,0:T(8,128)(2,1)S(1)}, bf16[128,256]{1,0:T(8,128)(2,1)}, u32[]{:S(2)}) copy-start(bf16[128,256]{1,0:T(8,128)(2,1)} %param.11) | copy-start | bytes 196612
  174.1 3.5 %copy-start = (bf16[64,4,32,128]{3,2,1,0:T(8,128)(2,1)S(1)}, bf16[64,4,32,128]{3,2,1,0:T(8,128)(2,1)}, u32[]{:S(2)}) copy-start(bf16[64,4,32,128]{3,2,1,0:T(8,128)(2,1)} %get-tuple-element.10) | copy-start | bytes 6291460
  179.7 0.8 copy-start.3
